TPU v7x, 256 devices: a whole 4x4x8 slice. The times are simulated.
256 devices in a mesh: rows: 16 (over y, x), pairs: 16 (over z, core).
Axes of the slice: x: 4, y: 4, z: 8, core: 2. Of those that a mesh axis runs over, the one named last changes fastest.
Arguments:
- latent: bfloat16 [32768, 6144], P('rows', 'pairs'), as said below
Outputs:
- rotated_latent: bfloat16 [32768, 6144], P('rows', 'pairs')
Inputs may be any that keep to these rules, and one draw needn't show every extreme that they name: `latent`: finite real entries.
All inputs are finite; a program needn't handle non-finite values.
Results may differ from a plain program's by a relative error of at most 0.0065.
Values may be sent and summed in bfloat16 or wider, within the bound.
A program may use at most 64 MiB of HBM per device.

v0:
```python
import math

import jax
import jax.numpy as jnp
from jax import lax
from jax.sharding import PartitionSpec as P

ROUNDS = 2
NS_ITERS = 2


def rows_for(lines, peers):
    spare = -len(lines) % peers
    return jnp.pad(lines, [(0, spare)] + [(0, 0)] * (lines.ndim - 1))


def joined_along(tiles, dim):
    dims = list(tiles.shape[1:])
    dims[dim] *= tiles.shape[0]
    return jnp.moveaxis(tiles, 0, dim).reshape(dims)


def from_everyone(shard, axis):
    copies = jnp.broadcast_to(shard, (lax.axis_size(axis), *shard.shape))
    return lax.all_to_all(copies, axis, split_axis=0, concat_axis=0, tiled=True)


def gathered_copies(shard, axis, dim):
    return joined_along(from_everyone(shard, axis), dim)


def in_blocks(shard, dim, peers):
    dims = shard.shape
    tiles = shard.reshape(*dims[:dim], peers, dims[dim] // peers, *dims[dim + 1 :])
    return jnp.moveaxis(tiles, dim, 0)


def sum_at_owner(shard, axis, dim):
    tiles = in_blocks(shard, dim, lax.axis_size(axis))
    arrived = lax.all_to_all(tiles, axis, split_axis=0, concat_axis=0, tiled=True)
    return arrived.sum(axis=0)


def sum_by_parts(shard, axes):
    padded = rows_for(shard, lax.axis_size(axes))
    whole = gathered_copies(sum_at_owner(padded, axes, 0), axes, 0)
    return lax.slice_in_dim(whole, 0, len(shard)).reshape(shard.shape)


def together(arrays, axis):
    ends = [0]
    for a in arrays:
        ends.append(ends[-1] + a.size)
    subtotal = sum_by_parts(jnp.concatenate([a.ravel() for a in arrays]), axis)
    return tuple((subtotal[b:e].reshape(a.shape) for a, b, e in zip(arrays, ends, ends[1:])))


def passed_along(shard, axis, by):
    peers = lax.axis_size(axis)
    return lax.ppermute(shard, axis, [(i, (i + by) % peers) for i in range(peers)])


def orthogonal(norms, cross):
    half = cross.shape[0]
    corr = cross / jnp.sqrt(norms[:half, None] * norms[None, half:])
    total = jnp.sqrt(2.0 * jnp.sum(corr * corr) + 1e-12)
    scaled = corr * (8.0 / total)
    empty = jnp.zeros((half, half), jnp.float32)
    upper = jnp.concatenate([empty, scaled], axis=1)
    lower = jnp.concatenate([-scaled.T, empty], axis=1)
    ident = jnp.eye(2 * half, dtype=jnp.float32)
    current = (ident + jnp.concatenate([upper, lower], axis=0)) * (1.5 / math.sqrt(65.0))
    for _ in range(NS_ITERS):
        inner = jnp.dot(current.T, current, precision=lax.Precision.HIGHEST)
        current = 1.5 * current - 0.5 * jnp.dot(current, inner, precision=lax.Precision.HIGHEST)
    return current.astype(jnp.bfloat16)


def rotor_of(window):
    half = window.shape[1] // 2
    cross = jnp.dot(window[:, :half].T, window[:, half:], preferred_element_type=jnp.float32)
    squares = jnp.sum(jnp.square(window.astype(jnp.float32)), axis=0)
    cross, squares = together((cross, squares), "rows")
    return orthogonal(squares, cross)


def local(latent):
    half = latent.shape[1] // 2
    window = latent
    for _ in range(ROUNDS):
        from_below = passed_along(window, "pairs", 1)
        from_above = passed_along(window, "pairs", -1)
        rotor = rotor_of(window)
        left_rotor = passed_along(rotor[:, :half], "pairs", 1)
        right_rotor = passed_along(rotor[:, half:], "pairs", -1)
        left_next = jnp.dot(from_below, left_rotor, preferred_element_type=jnp.float32).astype(
            jnp.bfloat16
        )
        right_next = jnp.dot(from_above, right_rotor, preferred_element_type=jnp.float32).astype(
            jnp.bfloat16
        )
        window = jnp.concatenate([left_next, right_next], axis=1)
    return window


def solution(mesh):
    return jax.shard_map(
        local,
        mesh=mesh,
        in_specs=(P("rows", "pairs"),),
        out_specs=P("rows", "pairs"),
        check_vma=False,
    )
```

profile of v0, /device:TPU:2, one launch (start us, length us, event | category | flops | bytes accessed | tf_op | source)
XLA Modules:
  0.0 99.8 jit_solution(6847051884363855654)
XLA Ops:
  0.0 1.9 %multiply_reduce_fusion.1 = f32[384]{0:T(512)S(1)} fusion(bf16[2048,384]{1,0:T(8,128)(2,1)} %param.1), kind=kLoop, calls=%fused_computation.1 | loop fusion | flops 2358912 | bytes 1574400 | tf_op jit(solution)/shard_map/reduce_sum | solution.py:82
  1.9 0.0 copy-done
  1.9 0.8 fusion.6
  2.7 0.1 reshape.40
  2.9 0.2 all_to_all.20
  3.1 14.0 %all_to_all.30 = f32[16,1,2328]{2,1,0:T(1,128)S(1)} all-to-all(f32[16,1,2328]{2,1,0:T(1,128)S(1)} %all_to_all.20), channel_id=1, replica_groups=mesh['rows'=16,'pairs'=16] {'rows'}, dimensions={0} | all-to-all | bytes 297984 | tf_op jit(solution)/shard_map/all_to_all | solution.py:40
  17.1 0.1 reduce_sum.55
  17.3 0.7 broadcast_in_dim.4
  18.0 4.8 %all-to-all-start.1 = ((f32[16,1,2328]{2,1,0:T(1,128)}), f32[16,1,2328]{2,1,0:T(1,128)S(1)}, u32[]{:S(2)}, u32[]{:S(2)}) async-start(f32[16,1,2328]{2,1,0:T(1,128)} %broadcast_in_dim.4), calls=%async_computation.1 | async-start | bytes 311296 | tf_op jit(solution)/shard_map/all_to_all | solution.py:25
  22.8 3.6 %collective-permute-start.3 = (bf16[2048,384]{1,0:T(8,128)(2,1)S(1)}, bf16[2048,384]{1,0:T(8,128)(2,1)}, u32[]{:S(2)}, u32[]{:S(2)}) collective-permute-start(bf16[2048,384]{1,0:T(8,128)(2,1)S(1)} %copy-done), channel_id=1, source_target_pairs={{0,15},{1,0},{2,1},{3,2},{4,3},{5,4},{6,5},{7,6},{8,7},{9,8},{10,9... | collective-permute-start | bytes 4718600 | tf_op jit(solution)/shard_map/ppermute | solution.py:60
  26.4 0.0 collective-permute-start.1
  26.4 3.3 %all-to-all-done.1 = f32[16,1,2328]{2,1,0:T(1,128)S(1)} async-done(((f32[16,1,2328]{2,1,0:T(1,128)}), f32[16,1,2328]{2,1,0:T(1,128)S(1)}, u32[]{:S(2)}, u32[]{:S(2)}) %all-to-all-start.1) | async-done | bytes 149024 | tf_op jit(solution)/shard_map/all_to_all | solution.py:25
  29.6 0.4 reduce.2
  30.0 0.1 reshape.41
  30.1 0.2 slice.50
  30.3 0.1 fusion.50
  30.4 0.7 multiply_reduce_fusion.3
  31.8 0.1 negate_bitcast_fusion.1
  31.9 0.1 copy.21
  32.1 1.3 %fusion.13 = f32[384,384]{1,0:T(8,128)S(1)} fusion(f32[192,192]{0,1:T(8,128)S(1)} %get-tuple-element.7, f32[192,192]{0,1:T(8,128)S(1)} %copy.21), kind=kOutput, calls=%fused_computation.32 | convolution fusion | flops 680804352 | bytes 884736 | tf_op jit(solution)/shard_map/dot_general | solution.py:74
  33.4 1.4 %fusion = f32[384,384]{0,1:T(8,128)S(1)} fusion(f32[384,384]{1,0:T(8,128)S(1)} %fusion.13, f32[192,192]{0,1:T(8,128)S(1)} %get-tuple-element.7, f32[192,192]{0,1:T(8,128)S(1)} %copy.21), kind=kOutput, calls=%fused_computation.12 | convolution fusion | flops 682426368 | bytes 1474560 | tf_op jit(solution)/shard_map/dot_general | solution.py:75
  34.8 1.3 %fusion.51 = f32[384,384]{1,0:T(8,128)S(1)} fusion(f32[384,384]{0,1:T(8,128)S(1)} %fusion), kind=kOutput, calls=%fused_computation.76 | convolution fusion | flops 679477248 | bytes 1179648 | tf_op jit(solution)/shard_map/dot_general | solution.py:74
  36.1 1.3 %fusion.5 = bf16[384,384]{0,1:T(8,128)(2,1)S(1)} fusion(f32[384,384]{0,1:T(8,128)S(1)} %fusion, f32[384,384]{1,0:T(8,128)S(1)} %fusion.51), kind=kOutput, calls=%fused_computation.17 | convolution fusion | flops 680067072 | bytes 1474560 | tf_op jit(solution)/shard_map/dot_general | solution.py:75
  37.5 2.7 %collective-permute-start.2 = (bf16[384,192]{0,1:T(8,128)(2,1)S(1)}, bf16[384,192]{0,1:T(8,128)(2,1)S(1)}, u32[]{:S(2)}, u32[]{:S(2)}) collective-permute-start(bf16[384,192]{0,1:T(8,128)(2,1)S(1)} %get-tuple-element.12), channel_id=1, source_target_pairs={{0,15},{1,0},{2,1},{3,2},{4,3},{5,4},{6,5},{7,6},{8,7},{9,8},{10,9... | collective-permute-start | bytes 442376 | tf_op jit(solution)/shard_map/ppermute | solution.py:60
  40.2 0.0 collective-permute-start
  40.2 5.7 %collective-permute-done.2 = bf16[384,192]{0,1:T(8,128)(2,1)S(1)} collective-permute-done((bf16[384,192]{0,1:T(8,128)(2,1)S(1)}, bf16[384,192]{0,1:T(8,128)(2,1)S(1)}, u32[]{:S(2)}, u32[]{:S(2)}) %collective-permute-start.2) | collective-permute-done | bytes 147488 | tf_op jit(solution)/shard_map/ppermute | solution.py:60
  45.9 0.0 collective-permute-done.3
  45.9 2.1 %convolution_convert_fusion.2 = bf16[192,2048]{1,0:T(8,128)(2,1)S(1)} fusion(bf16[384,192]{0,1:T(8,128)(2,1)S(1)} %collective-permute-done.2, bf16[2048,384]{1,0:T(8,128)(2,1)} %collective-permute-done.3), kind=kOutput, calls=%fused_computation.4 | convolution fusion | flops 302383104 | bytes 2506752 | tf_op jit(solution)/shard_map/dot_general | solution.py:99
  48.0 1.0 collective-permute-done
  49.0 0.0 collective-permute-done.1
  49.0 2.1 %convolution_convert_fusion.3 = bf16[192,2048]{1,0:T(8,128)(2,1)S(1)} fusion(bf16[384,192]{0,1:T(8,128)(2,1)S(1)} %collective-permute-done, bf16[2048,384]{1,0:T(8,128)(2,1)} %collective-permute-done.1), kind=kOutput, calls=%fused_computation.5 | convolution fusion | flops 302383104 | bytes 2506752 | tf_op jit(solution)/shard_map/dot_general | solution.py:96
  51.1 0.4 fusion.52
  51.5 0.1 reshape.42
  51.6 0.4 multiply_reduce_fusion
  52.0 0.2 all_to_all.23
  52.3 13.8 %all_to_all.31 = f32[16,1,2328]{2,1,0:T(1,128)S(1)} all-to-all(f32[16,1,2328]{2,1,0:T(1,128)S(1)} %all_to_all.23), channel_id=1, replica_groups=mesh['rows'=16,'pairs'=16] {'rows'}, dimensions={0} | all-to-all | bytes 297984 | tf_op jit(solution)/shard_map/all_to_all | solution.py:40
  66.1 0.1 reduce_sum.58
  66.2 0.7 broadcast_in_dim.5
  67.0 4.8 %all-to-all-start.3 = ((f32[16,1,2328]{2,1,0:T(1,128)}), f32[16,1,2328]{2,1,0:T(1,128)S(1)}, u32[]{:S(2)}, u32[]{:S(2)}) async-start(f32[16,1,2328]{2,1,0:T(1,128)} %broadcast_in_dim.5), calls=%async_computation.3 | async-start | bytes 311296 | tf_op jit(solution)/shard_map/all_to_all | solution.py:25
  71.7 0.2 pad_maximum_fusion
  71.9 1.6 %collective-permute-start.6 = (bf16[2048,384]{0,1:T(8,128)(2,1)S(1)}, bf16[2048,384]{0,1:T(8,128)(2,1)}, u32[]{:S(2)}, u32[]{:S(2)}) collective-permute-start(bf16[2048,384]{0,1:T(8,128)(2,1)S(1)} %pad_maximum_fusion), channel_id=1, source_target_pairs={{0,15},{1,0},{2,1},{3,2},{4,3},{5,4},{6,5},{7,6},{8,7},{9,8},{10,9... | collective-permute-start | bytes 4718600 | tf_op jit(solution)/shard_map/ppermute | solution.py:60
  73.5 0.0 collective-permute-start.4
  73.5 5.1 %all-to-all-done.3 = f32[16,1,2328]{2,1,0:T(1,128)S(1)} async-done(((f32[16,1,2328]{2,1,0:T(1,128)}), f32[16,1,2328]{2,1,0:T(1,128)S(1)}, u32[]{:S(2)}, u32[]{:S(2)}) %all-to-all-start.3) | async-done | bytes 149024 | tf_op jit(solution)/shard_map/all_to_all | solution.py:25
  78.6 0.4 reduce.4
  79.0 0.1 reshape.43
  79.1 0.2 slice.56
  79.3 0.1 fusion.49
  79.4 0.7 multiply_reduce_fusion.2
  80.8 0.1 negate_bitcast_fusion
  80.9 0.1 copy.22
  81.0 1.3 %fusion.10 = f32[384,384]{1,0:T(8,128)S(1)} fusion(f32[192,192]{0,1:T(8,128)S(1)} %get-tuple-element.5, f32[192,192]{0,1:T(8,128)S(1)} %copy.22), kind=kOutput, calls=%fused_computation.29 | convolution fusion | flops 680804352 | bytes 884736 | tf_op jit(solution)/shard_map/dot_general | solution.py:74
  82.4 1.4 %fusion.2 = f32[384,384]{0,1:T(8,128)S(1)} fusion(f32[384,384]{1,0:T(8,128)S(1)} %fusion.10, f32[192,192]{0,1:T(8,128)S(1)} %get-tuple-element.5, f32[192,192]{0,1:T(8,128)S(1)} %copy.22), kind=kOutput, calls=%fused_computation.14 | convolution fusion | flops 682426368 | bytes 1474560 | tf_op jit(solution)/shard_map/dot_general | solution.py:75
  83.8 1.3 %fusion.53 = f32[384,384]{1,0:T(8,128)S(1)} fusion(f32[384,384]{0,1:T(8,128)S(1)} %fusion.2), kind=kOutput, calls=%fused_computation.78 | convolution fusion | flops 679477248 | bytes 1179648 | tf_op jit(solution)/shard_map/dot_general | solution.py:74
  85.1 1.3 %fusion.4 = bf16[384,384]{0,1:T(8,128)(2,1)S(1)} fusion(f32[384,384]{0,1:T(8,128)S(1)} %fusion.2, f32[384,384]{1,0:T(8,128)S(1)} %fusion.53), kind=kOutput, calls=%fused_computation.16 | convolution fusion | flops 680067072 | bytes 1474560 | tf_op jit(solution)/shard_map/dot_general | solution.py:75
  86.5 1.0 collective-permute-start.7
  87.5 0.0 collective-permute-start.5
  87.5 5.5 %collective-permute-done.7 = bf16[384,192]{0,1:T(8,128)(2,1)S(1)} collective-permute-done((bf16[384,192]{0,1:T(8,128)(2,1)S(1)}, bf16[384,192]{0,1:T(8,128)(2,1)S(1)}, u32[]{:S(2)}, u32[]{:S(2)}) %collective-permute-start.7) | collective-permute-done | bytes 147488 | tf_op jit(solution)/shard_map/ppermute | solution.py:60
  93.0 0.0 collective-permute-done.6
  93.0 2.0 %convolution_convert_fusion = bf16[2048,192]{0,1:T(8,128)(2,1)S(1)} fusion(bf16[384,192]{0,1:T(8,128)(2,1)S(1)} %collective-permute-done.7, bf16[2048,384]{0,1:T(8,128)(2,1)} %collective-permute-done.6), kind=kOutput, calls=%fused_computation.2 | convolution fusion | flops 302383104 | bytes 2506752 | tf_op jit(solution)/shard_map/dot_general | solution.py:99
  95.0 1.1 %collective-permute-done.5 = bf16[384,192]{0,1:T(8,128)(2,1)S(1)} collective-permute-done((bf16[384,192]{0,1:T(8,128)(2,1)S(1)}, bf16[384,192]{0,1:T(8,128)(2,1)S(1)}, u32[]{:S(2)}, u32[]{:S(2)}) %collective-permute-start.5) | collective-permute-done | bytes 147488 | tf_op jit(solution)/shard_map/ppermute | solution.py:60
  96.1 0.0 collective-permute-done.4
  96.1 2.0 %convolution_convert_fusion.1 = bf16[2048,192]{0,1:T(8,128)(2,1)S(1)} fusion(bf16[384,192]{0,1:T(8,128)(2,1)S(1)} %collective-permute-done.5, bf16[2048,384]{0,1:T(8,128)(2,1)} %collective-permute-done.4), kind=kOutput, calls=%fused_computation.3 | convolution fusion | flops 302383104 | bytes 2506752 | tf_op jit(solution)/shard_map/dot_general | solution.py:96
  98.1 0.1 pad_maximum_fusion.1
  98.2 1.6 %copy.18 = bf16[2048,384]{1,0:T(8,128)(2,1)} copy(bf16[2048,384]{0,1:T(8,128)(2,1)S(1)} %pad_maximum_fusion.1) | data formatting | bytes 3145728 | tf_op jit(solution)/shard_map/concatenate | solution.py:102
  (5 shorter events, 0.1 us)
Async XLA Ops:
  0.0 1.9 %copy-start = (bf16[2048,384]{1,0:T(8,128)(2,1)S(1)}, bf16[2048,384]{1,0:T(8,128)(2,1)}, u32[]{:S(2)}) copy-start(bf16[2048,384]{1,0:T(8,128)(2,1)} %param.1) | copy-start | bytes 4718596
  18.0 11.6 %all-to-all-start.1 = ((f32[16,1,2328]{2,1,0:T(1,128)}), f32[16,1,2328]{2,1,0:T(1,128)S(1)}, u32[]{:S(2)}, u32[]{:S(2)}) async-start(f32[16,1,2328]{2,1,0:T(1,128)} %broadcast_in_dim.4), calls=%async_computation.1 | async-start | bytes 311296 | tf_op jit(solution)/shard_map/all_to_all | solution.py:25
  22.8 23.1 %collective-permute-start.3 = (bf16[2048,384]{1,0:T(8,128)(2,1)S(1)}, bf16[2048,384]{1,0:T(8,128)(2,1)}, u32[]{:S(2)}, u32[]{:S(2)}) collective-permute-start(bf16[2048,384]{1,0:T(8,128)(2,1)S(1)} %copy-done), channel_id=1, source_target_pairs={{0,15},{1,0},{2,1},{3,2},{4,3},{5,4},{6,5},{7,6},{8,7},{9,8},{10,9... | collective-permute-start | bytes 4718600 | tf_op jit(solution)/shard_map/ppermute | solution.py:60
  26.4 22.6 %collective-permute-start.1 = (bf16[2048,384]{1,0:T(8,128)(2,1)S(1)}, bf16[2048,384]{1,0:T(8,128)(2,1)}, u32[]{:S(2)}, u32[]{:S(2)}) collective-permute-start(bf16[2048,384]{1,0:T(8,128)(2,1)S(1)} %copy-done), channel_id=1, source_target_pairs={{0,1},{1,2},{2,3},{3,4},{4,5},{5,6},{6,7},{7,8},{8,9},{9,10},{10,1... | collective-permute-start | bytes 4718600 | tf_op jit(solution)/shard_map/ppermute | solution.py:60
  37.5 8.4 %collective-permute-start.2 = (bf16[384,192]{0,1:T(8,128)(2,1)S(1)}, bf16[384,192]{0,1:T(8,128)(2,1)S(1)}, u32[]{:S(2)}, u32[]{:S(2)}) collective-permute-start(bf16[384,192]{0,1:T(8,128)(2,1)S(1)} %get-tuple-element.12), channel_id=1, source_target_pairs={{0,15},{1,0},{2,1},{3,2},{4,3},{5,4},{6,5},{7,6},{8,7},{9,8},{10,9... | collective-permute-start | bytes 442376 | tf_op jit(solution)/shard_map/ppermute | solution.py:60
  40.2 8.8 %collective-permute-start = (bf16[384,192]{0,1:T(8,128)(2,1)S(1)}, bf16[384,192]{0,1:T(8,128)(2,1)S(1)}, u32[]{:S(2)}, u32[]{:S(2)}) collective-permute-start(bf16[384,192]{0,1:T(8,128)(2,1)S(1)} %get-tuple-element.11), channel_id=1, source_target_pairs={{0,1},{1,2},{2,3},{3,4},{4,5},{5,6},{6,7},{7,8},{8,9},{9,10},{10,1... | collective-permute-start | bytes 442376 | tf_op jit(solution)/shard_map/ppermute | solution.py:60
  67.0 11.6 %all-to-all-start.3 = ((f32[16,1,2328]{2,1,0:T(1,128)}), f32[16,1,2328]{2,1,0:T(1,128)S(1)}, u32[]{:S(2)}, u32[]{:S(2)}) async-start(f32[16,1,2328]{2,1,0:T(1,128)} %broadcast_in_dim.5), calls=%async_computation.3 | async-start | bytes 311296 | tf_op jit(solution)/shard_map/all_to_all | solution.py:25
  71.9 21.1 %collective-permute-start.6 = (bf16[2048,384]{0,1:T(8,128)(2,1)S(1)}, bf16[2048,384]{0,1:T(8,128)(2,1)}, u32[]{:S(2)}, u32[]{:S(2)}) collective-permute-start(bf16[2048,384]{0,1:T(8,128)(2,1)S(1)} %pad_maximum_fusion), channel_id=1, source_target_pairs={{0,15},{1,0},{2,1},{3,2},{4,3},{5,4},{6,5},{7,6},{8,7},{9,8},{10,9... | collective-permute-start | bytes 4718600 | tf_op jit(solution)/shard_map/ppermute | solution.py:60
  73.5 22.6 %collective-permute-start.4 = (bf16[2048,384]{0,1:T(8,128)(2,1)S(1)}, bf16[2048,384]{0,1:T(8,128)(2,1)}, u32[]{:S(2)}, u32[]{:S(2)}) collective-permute-start(bf16[2048,384]{0,1:T(8,128)(2,1)S(1)} %pad_maximum_fusion), channel_id=1, source_target_pairs={{0,1},{1,2},{2,3},{3,4},{4,5},{5,6},{6,7},{7,8},{8,9},{9,10},{10,1... | collective-permute-start | bytes 4718600 | tf_op jit(solution)/shard_map/ppermute | solution.py:60
  86.5 6.5 %collective-permute-start.7 = (bf16[384,192]{0,1:T(8,128)(2,1)S(1)}, bf16[384,192]{0,1:T(8,128)(2,1)S(1)}, u32[]{:S(2)}, u32[]{:S(2)}) collective-permute-start(bf16[384,192]{0,1:T(8,128)(2,1)S(1)} %get-tuple-element.10), channel_id=1, source_target_pairs={{0,15},{1,0},{2,1},{3,2},{4,3},{5,4},{6,5},{7,6},{8,7},{9,8},{10,9... | collective-permute-start | bytes 442376 | tf_op jit(solution)/shard_map/ppermute | solution.py:60
  87.5 8.6 %collective-permute-start.5 = (bf16[384,192]{0,1:T(8,128)(2,1)S(1)}, bf16[384,192]{0,1:T(8,128)(2,1)S(1)}, u32[]{:S(2)}, u32[]{:S(2)}) collective-permute-start(bf16[384,192]{0,1:T(8,128)(2,1)S(1)} %get-tuple-element.9), channel_id=1, source_target_pairs={{0,1},{1,2},{2,3},{3,4},{4,5},{5,6},{6,7},{7,8},{8,9},{9,10},{10,1... | collective-permute-start | bytes 442376 | tf_op jit(solution)/shard_map/ppermute | solution.py:60
where the time goes:
time: 100 us; the launch traced here: 99.8 us
  blocking collectives  27.9 us (28%)
  waiting for transfers between devices  21.7 us (22%)
  matrix products  20.1 us (20%)
  starting transfers between devices  18.4 us (18%)
  other arithmetic  5.23 us (5%)
  local copies, waits for them, and re-layouts  4.88 us (5%)
  between operations  1.64 us (2%)
    all_to_all x2, blocking collectives, sum_at_owner(): lax.all_to_all(tiles, axis, split_axis=0, concat_axis=0, tiled=True)  27.9 us
    ppermute x8, waiting for transfers between devices, passed_along(): lax.ppermute(shard, axis, [(i, (i + by) % peers) for i in range(peers)])  13.3 us
    all_to_all x2, starting transfers between devices, from_everyone(): return lax.all_to_all(copies, axis, split_axis=0, concat_axis=0, tiled=True)  9.53 us
    ppermute x8, starting transfers between devices, passed_along(): lax.ppermute(shard, axis, [(i, (i + by) % peers) for i in range(peers)])  8.86 us
    all_to_all x2, waiting for transfers between devices, from_everyone(): return lax.all_to_all(copies, axis, split_axis=0, concat_axis=0, tiled=True)  8.37 us
    dot_general x4, matrix products, orthogonal(): jnp.dot(current, inner, precision=lax.Precision.HIGHEST)  5.5 us
    dot_general x4, matrix products, orthogonal(): inner = jnp.dot(current.T, current, precision=lax.Precision.HIGHEST)  5.22 us
    dot_general x2, matrix products, local(): jnp.dot(from_above, right_rotor, preferred_element_type=jnp.float32)  4.1 us
  transfers between devices with their start and end apart: 10, of which 6 were waited for; matrix products, arithmetic and copies ran while one was open for 19% of the time, Pallas kernels for 0%

commit v1 on v0

v1 whole, which is shorter than its diff:
```python
import functools
import math

import jax
import jax.numpy as jnp
from jax import lax
from jax.experimental import pallas as pl
from jax.experimental.pallas import tpu as pltpu
from jax.sharding import PartitionSpec as P

BF = jnp.bfloat16
F32 = jnp.float32
BLK = 192
WIDE = 2 * BLK
CHUNKS = 8
MESH = pl.DeviceIdType.MESH


def polynomial():
    a = 1.5 / math.sqrt(65.0)
    t = a * a
    f = [2.25, -2.4375, 1.6875, -0.5625, 0.0625]
    c = []
    for k in range(5):
        c.append(a * sum(f[n] * math.comb(n, k) * t ** (n - k) for n in range(k, 5)))
    return t, c


def dot(a, b):
    return jnp.dot(a, b, preferred_element_type=F32)


def dot_nt(a, b):
    return lax.dot_general(a, b, (((1,), (1,)), ((), ())), preferred_element_type=F32)


def dot_tn(a, b):
    return lax.dot_general(a, b, (((0,), (0,)), ((), ())), preferred_element_type=F32)


def iota(shape, dim):
    return lax.broadcasted_iota(jnp.int32, shape, dim)


def series(h, c, eye):
    hb = h.astype(BF)
    h2 = dot(hb, hb)
    rest = c[1] * h + c[2] * h2 + dot(h2.astype(BF), (c[3] * h + c[4] * h2).astype(BF))
    return jnp.where(eye, rest + c[0], rest), rest.astype(BF)


def left_columns(cw, ct):
    t, c = polynomial()
    cb = cw.astype(BF)
    row, lane = iota((256, 256), 0), iota((256, 256), 1)
    q1, p1 = series(t * dot_nt(cb, cb), c, (row == lane) & (lane < BLK))
    kt = c[0] * ct + dot(ct.astype(BF), p1)
    return q1, -kt


def right_columns(cw, ct):
    t, c = polynomial()
    cb, ctb = cw.astype(BF), ct.astype(BF)
    row, lane = iota((256, 256), 0), iota((256, 256), 1)
    q2, p2 = series(t * dot_nt(ctb, ctb), c, (row == lane) & (lane >= 64))
    k = c[0] * cw + dot(cb, p2)
    return k, q2


def with_norms(gram, left_sq, right_sq):
    row, lane = iota((BLK, 256), 0), iota((BLK, 256), 1)
    nl = jnp.sum(jnp.where(lane == row, left_sq, 0.0), axis=1, keepdims=True)
    nr = jnp.sum(jnp.where(lane == row + 64, right_sq, 0.0), axis=1, keepdims=True)
    side = jnp.where(lane == 0, nl, jnp.where(lane == 2, nr, 0.0))
    return jnp.where(lane >= 64, gram, side)


def step_of(total):
    row, lane = iota((BLK, 256), 0), iota((BLK, 256), 1)
    nl = total[:, 0:1]
    nr = jnp.sum(jnp.where(lane == row + 64, total[:, 2:3], 0.0), axis=0, keepdims=True)
    corr = jnp.where(lane >= 64, total * lax.rsqrt(nl) * lax.rsqrt(nr), 0.0)
    square = jnp.sum(jnp.sum(corr * corr, axis=0, keepdims=True), axis=1, keepdims=True)
    return corr * (8.0 * lax.rsqrt(2.0 * square + 1e-12))


def squared(c):
    return jnp.concatenate([c, jnp.zeros((64, 256), F32)], axis=0)


def rolled(x):
    return pltpu.roll(x, 64, axis=1)


def kernel(
    nx, ny, npos,
    w_hbm, out_hbm,
    w, own_l, own_r, in_l, in_r, far_l, far_r, out_v,
    ql, qr, wl, wr, acc, part, got, c_own, c_prev, c_next,
    load_sem, store_sem, sum_send, sum_recv, mv_send, mv_recv, c_send, c_recv,
):
    r, p = lax.axis_index("rows"), lax.axis_index("pairs")
    x, y = lax.rem(r, nx), lax.div(r, nx)
    nxt, prv = lax.rem(p + 1, npos), lax.rem(p + npos - 1, npos)
    rows = w_hbm.shape[0]
    ch = rows // CHUNKS
    g = ch // 2

    def along(axis, k):
        if axis == 0:
            return (y * nx + lax.rem(x + k, nx), p)
        return (lax.rem(y + k, ny) * nx + x, p)

    ring = (nx, ny)
    peers = [along(a, k) for a in (0, 1) for k in range(1, ring[a])] + [(r, nxt), (r, prv)]

    loads = [
        pltpu.make_async_copy(
            w_hbm.at[pl.ds(c * ch, ch)], w.at[pl.ds(c * ch, ch)], load_sem.at[c]
        )
        for c in range(CHUNKS)
    ]
    for copy in loads:
        copy.start()
    barrier = pltpu.get_barrier_semaphore()
    for peer in peers:
        pl.semaphore_signal(barrier, inc=1, device_id=peer, device_id_type=MESH)

    started = []

    def remote(src, dst, send, recv, target):
        copy = pltpu.make_async_remote_copy(
            src_ref=src, dst_ref=dst, send_sem=send, recv_sem=recv,
            device_id=target, device_id_type=MESH,
        )
        copy.start()
        started.append(copy)
        return copy

    def summed(rnd, payload):
        flight = {}

        def send(phase, h, value):
            axis = (phase + h) % 2
            part[rnd, phase, h] = value.astype(BF)
            flight[phase, h] = [
                remote(
                    part.at[rnd, phase, h], got.at[rnd, phase, h, k - 1],
                    sum_send.at[rnd, phase, h, k - 1], sum_recv.at[rnd, phase, h, k - 1],
                    along(axis, k),
                )
                for k in range(1, ring[axis])
            ]

        def collect(phase, h):
            total = part[rnd, phase, h].astype(F32)
            for k, copy in enumerate(flight[phase, h]):
                copy.wait_recv()
                total = total + got[rnd, phase, h, k].astype(F32)
            return total

        half = BLK // 2
        send(0, 0, payload[:half])
        send(0, 1, payload[half:])
        send(1, 0, collect(0, 0))
        send(1, 1, collect(0, 1))
        return jnp.concatenate([collect(1, 0), collect(1, 1)], axis=0)

    acc[0] = jnp.zeros((256, 256), F32)
    sq = jnp.zeros((8, WIDE), F32)
    for c in range(CHUNKS):
        loads[c].wait()
        block = w[pl.ds(c * ch, ch)]
        acc[0] += dot_tn(block[:, :256], block[:, 128:])
        wide = block.astype(F32)
        sq = sq + jnp.sum((wide * wide).reshape(ch // 8, 8, WIDE), axis=0)
    sq = jnp.sum(sq, axis=0, keepdims=True)
    payload = with_norms(acc[0, :BLK], sq[:, :256], sq[:, 128:])

    pl.semaphore_wait(barrier, len(peers))
    cw = squared(step_of(summed(0, payload)))
    ct = cw.T
    q1, nkt = left_columns(cw, ct)
    k, q2 = right_columns(cw, ct)
    for rows_of, value in ((pl.ds(0, BLK), q1[:BLK]), (pl.ds(BLK, BLK), nkt[64:])):
        ql[0, rows_of] = value.astype(BF)
        ql[1, rows_of, :128] = value[:, :128].astype(BF)
        ql[1, rows_of, 128:] = rolled(value[:, 128:]).astype(BF)
    for rows_of, value in ((pl.ds(0, BLK), k[:BLK]), (pl.ds(BLK, BLK), q2[64:])):
        qr[0, rows_of] = value.astype(BF)
        qr[1, rows_of, :128] = rolled(value[:, :128]).astype(BF)
        qr[1, rows_of, 128:] = value[:, 128:].astype(BF)

    first = []
    for c in range(CHUNKS):
        top, low = w[pl.ds(c * ch, g)], w[pl.ds(c * ch + g, g)]
        a, b = dot(top, ql[0]), dot(low, ql[1])
        own_l[c, :g] = a[:, :128].astype(BF)
        own_l[c, g : 2 * g] = b[:, :128].astype(BF)
        own_l[c, 2 * g :] = (a[:, 128:] + b[:, 128:]).astype(BF)
        a, b = dot(top, qr[0]), dot(low, qr[1])
        own_r[c, :g] = a[:, 128:].astype(BF)
        own_r[c, g : 2 * g] = b[:, 128:].astype(BF)
        own_r[c, 2 * g :] = (a[:, :128] + b[:, :128]).astype(BF)
        first.append((
            remote(own_l.at[c], in_l.at[c], mv_send.at[0, c], mv_recv.at[0, c], (r, nxt)),
            remote(own_r.at[c], in_r.at[c], mv_send.at[1, c], mv_recv.at[1, c], (r, prv)),
        ))

    acc[0] = jnp.zeros((256, 256), F32)
    acc[1] = jnp.zeros((256, 256), F32)
    sq_l = [jnp.zeros((8, 128), F32), jnp.zeros((8, 128), F32)]
    sq_r = [jnp.zeros((8, 128), F32), jnp.zeros((8, 128), F32)]
    second = []

    def squares(total, block):
        wide = block.astype(F32)
        wide = wide * wide
        a = jnp.sum(wide[: 2 * g].reshape(2 * g // 8, 8, 128), axis=0)
        b = jnp.sum(wide[2 * g :].reshape(g // 8, 8, 128), axis=0)
        return [total[0] + a, total[1] + b]

    for c in range(CHUNKS):
        first[c][0].wait_recv()
        first[c][1].wait_recv()
        second.append((
            remote(in_l.at[c], far_l.at[c], mv_send.at[2, c], mv_recv.at[2, c], (r, nxt)),
            remote(in_r.at[c], far_r.at[c], mv_send.at[3, c], mv_recv.at[3, c], (r, prv)),
        ))
        left, right = in_l[c], in_r[c]
        lb, rb = left[2 * g :], right[2 * g :]
        for half in range(2):
            a = jnp.concatenate([left[half * g : half * g + g], lb], axis=1)
            b = jnp.concatenate([rb, right[half * g : half * g + g]], axis=1)
            acc[half] += dot_tn(a, b)
        sq_l = squares(sq_l, left)
        sq_r = squares(sq_r, right)

    def folded(total):
        a, b = (jnp.sum(v, axis=0, keepdims=True) for v in total)
        return a, b + rolled(b)

    la, lb = folded(sq_l)
    ra, rb = folded(sq_r)
    lower = jnp.concatenate([acc[1, :128], acc[1, BLK:]], axis=0)
    lower = jnp.concatenate([rolled(lower[:, :128]), lower[:, 128:]], axis=1)
    payload = with_norms(
        acc[0, :BLK] + lower,
        jnp.concatenate([la, lb], axis=1),
        jnp.concatenate([rb, ra], axis=1),
    )
    c_own[...] = step_of(summed(1, payload)).astype(BF)
    up = remote(c_own, c_prev, c_send.at[0], c_recv.at[0], (r, nxt))
    down = remote(c_own, c_next, c_send.at[1], c_recv.at[1], (r, prv))

    up.wait_recv()
    cw = squared(c_prev[...].astype(F32))
    q1, nkt = left_columns(cw, cw.T)
    wl[0, :256] = q1.astype(BF)
    wl[1, :128] = q1[:128].astype(BF)
    wl[1, 128:192] = q1[192:].astype(BF)
    wl[1, 192:256] = q1[128:192].astype(BF)
    wl[0, 256:] = nkt.astype(BF)
    wl[1, 256:320] = nkt[64:128].astype(BF)
    wl[1, 320:384] = nkt[:64].astype(BF)
    wl[1, 384:] = nkt[128:].astype(BF)
    down.wait_recv()
    cw = squared(c_next[...].astype(F32))
    k, q2 = right_columns(cw, cw.T)
    wr[0, :256] = k.astype(BF)
    wr[1, :128] = k[:128].astype(BF)
    wr[1, 128:192] = k[192:].astype(BF)
    wr[1, 192:256] = k[128:192].astype(BF)
    wr[0, 256:] = q2.astype(BF)
    wr[1, 256:320] = q2[64:128].astype(BF)
    wr[1, 320:384] = q2[:64].astype(BF)
    wr[1, 384:] = q2[128:].astype(BF)

    stores = []
    for c in range(CHUNKS):
        second[c][0].wait_recv()
        second[c][1].wait_recv()
        for half in range(2):
            part_of = pl.ds(half * g, g)
            b_of = pl.ds(2 * g, g)
            to_left = jnp.concatenate(
                [far_l[c, part_of], far_l[c, b_of], own_r[c, b_of], own_r[c, part_of]], axis=1
            )
            to_right = jnp.concatenate(
                [own_l[c, part_of], own_l[c, b_of], far_r[c, b_of], far_r[c, part_of]], axis=1
            )
            a, b = dot(to_left, wl[half]), dot(to_right, wr[half])
            rows_of = pl.ds(c * ch + half * g, g)
            out_v[rows_of, :128] = a[:, :128].astype(BF)
            out_v[rows_of, 128:256] = (a[:, 128:] + b[:, :128]).astype(BF)
            out_v[rows_of, 256:] = b[:, 128:].astype(BF)
        store = pltpu.make_async_copy(
            out_v.at[pl.ds(c * ch, ch)], out_hbm.at[pl.ds(c * ch, ch)], store_sem.at[c]
        )
        store.start()
        stores.append(store)
    for copy in started:
        copy.wait_send()
    for store in stores:
        store.wait()


def local(nx, ny, npos, latent):
    rows = latent.shape[0]
    g = rows // CHUNKS // 2
    packed = pltpu.VMEM((CHUNKS, 3 * g, 128), BF)
    return pl.pallas_call(
        functools.partial(kernel, nx, ny, npos),
        out_shape=jax.ShapeDtypeStruct(latent.shape, BF),
        in_specs=[pl.BlockSpec(memory_space=pl.ANY)],
        out_specs=pl.BlockSpec(memory_space=pl.ANY),
        scratch_shapes=[
            pltpu.VMEM((rows, WIDE), BF),
            packed, packed, packed, packed, packed, packed,
            pltpu.VMEM((rows, WIDE), BF),
            pltpu.VMEM((2, WIDE, 256), BF),
            pltpu.VMEM((2, WIDE, 256), BF),
            pltpu.VMEM((2, 512, 256), BF),
            pltpu.VMEM((2, 512, 256), BF),
            pltpu.VMEM((2, 256, 256), F32),
            pltpu.VMEM((2, 2, 2, BLK // 2, 256), BF),
            pltpu.VMEM((2, 2, 2, max(nx, ny) - 1, BLK // 2, 256), BF),
            pltpu.VMEM((BLK, 256), BF),
            pltpu.VMEM((BLK, 256), BF),
            pltpu.VMEM((BLK, 256), BF),
            pltpu.SemaphoreType.DMA((CHUNKS,)),
            pltpu.SemaphoreType.DMA((CHUNKS,)),
            pltpu.SemaphoreType.DMA((2, 2, 2, max(nx, ny) - 1)),
            pltpu.SemaphoreType.DMA((2, 2, 2, max(nx, ny) - 1)),
            pltpu.SemaphoreType.DMA((4, CHUNKS)),
            pltpu.SemaphoreType.DMA((4, CHUNKS)),
            pltpu.SemaphoreType.DMA((2,)),
            pltpu.SemaphoreType.DMA((2,)),
        ],
        compiler_params=pltpu.CompilerParams(
            collective_id=0, has_side_effects=True, vmem_limit_bytes=40 * 1024 * 1024
        ),
    )(latent)


def solution(mesh):
    side = math.isqrt(mesh.shape["rows"])
    return jax.shard_map(
        functools.partial(local, side, mesh.shape["rows"] // side, mesh.shape["pairs"]),
        mesh=mesh,
        in_specs=(P("rows", "pairs"),),
        out_specs=P("rows", "pairs"),
        check_vma=False,
    )
```

time: 100 us -> 54.1 us (0.54)
  the two profiles are of different devices: /device:TPU:2 before, /device:TPU:97 now
where the time goes in v1:
time: 54.1 us; the launch traced here: 54 us
  Pallas kernels  51.5 us (95%)
  local copies, waits for them, and re-layouts  2.55 us (5%)
    pallas_call x1, Pallas kernels, local(): pl.pallas_call(functools.partial(kernel, nx, ny, npos), out_shape=jax.Sha...  51.5 us
    unnamed x3, local copies, waits for them, and re-layouts  2.55 us

profile of v1, /device:TPU:97, one launch (start us, length us, event | category | flops | bytes accessed | tf_op | source)
XLA Modules:
  0.0 54.0 jit_solution(15782993943933811427)
XLA Ops:
  0.0 0.0 copy-start
  0.0 1.4 %copy-done = bf16[2048,384]{1,0:T(8,128)(2,1)S(1)} copy-done((bf16[2048,384]{1,0:T(8,128)(2,1)S(1)}, bf16[2048,384]{1,0:T(8,128)(2,1)}, u32[]{:S(2)}) %copy-start) | copy-done | bytes 1572888
  1.4 51.5 %shard_map.17 = bf16[2048,384]{1,0:T(8,128)(2,1)S(1)} custom-call(bf16[2048,384]{1,0:T(8,128)(2,1)S(1)} %copy-done), custom_call_target="tpu_custom_call" | custom-call | tf_op jit(solution)/shard_map/pallas_call | solution.py:312
  52.9 1.1 %copy.3 = bf16[2048,384]{1,0:T(8,128)(2,1)} copy(bf16[2048,384]{1,0:T(8,128)(2,1)S(1)} %shard_map.17) | data formatting | bytes 3145728
Async XLA Ops:
  0.0 1.4 %copy-start = (bf16[2048,384]{1,0:T(8,128)(2,1)S(1)}, bf16[2048,384]{1,0:T(8,128)(2,1)}, u32[]{:S(2)}) copy-start(bf16[2048,384]{1,0:T(8,128)(2,1)} %w_hbm.1) | copy-start | bytes 4718596

commit v2 on v1

v2 whole, which is shorter than its diff:
```python
import functools
import math

import jax
import jax.numpy as jnp
from jax import lax
from jax.experimental import pallas as pl
from jax.experimental.pallas import tpu as pltpu
from jax.sharding import PartitionSpec as P

BF = jnp.bfloat16
F32 = jnp.float32
BLK = 192
WIDE = 2 * BLK
CHUNKS = 8
PRE = 4
PACK = 288
SUM = 304
PIECES = ((0, 0, 80), (0, 80, 64), (1, 144, 80), (1, 224, 80))
ORDER = (0, 2, 1, 3)
MESH = pl.DeviceIdType.MESH


def polynomial():
    a = 1.5 / math.sqrt(65.0)
    t = a * a
    f = [2.25, -2.4375, 1.6875, -0.5625, 0.0625]
    c = []
    for k in range(5):
        c.append(a * sum(f[n] * math.comb(n, k) * t ** (n - k) for n in range(k, 5)))
    return t, c


def dot(a, b):
    return jnp.dot(a, b, preferred_element_type=F32)


def dot_nt(a, b):
    return lax.dot_general(a, b, (((1,), (1,)), ((), ())), preferred_element_type=F32)


def dot_tn(a, b):
    return lax.dot_general(a, b, (((0,), (0,)), ((), ())), preferred_element_type=F32)


def iota(shape, dim):
    return lax.broadcasted_iota(jnp.int32, shape, dim)


def series(h, c, full, eye):
    hb = h.astype(BF)
    h2 = dot(hb, full(hb))
    rest = c[1] * h + c[2] * h2 + dot(h2.astype(BF), full((c[3] * h + c[4] * h2).astype(BF)))
    return jnp.where(eye, rest + c[0], rest), full(rest.astype(BF))


def below(x):
    return jnp.concatenate([x, jnp.zeros((64, 256), x.dtype)], axis=0)


def above(x):
    return jnp.concatenate([jnp.zeros((64, 256), x.dtype), x], axis=0)


def left_columns(cw):
    t, c = polynomial()
    cb = cw.astype(BF)
    row, lane = iota((BLK, 256), 0), iota((BLK, 256), 1)
    q1, p1 = series(t * dot_nt(cb, below(cb)), c, below, row == lane)
    ct = below(cw).T[64:]
    return q1, -(c[0] * ct + dot(ct.astype(BF), p1))


def right_columns(cw):
    t, c = polynomial()
    cb = cw.astype(BF)
    ctb = below(cw).T[64:].astype(BF)
    row, lane = iota((BLK, 256), 0), iota((BLK, 256), 1)
    q2, p2 = series(t * dot_nt(ctb, above(ctb)), c, above, row + 64 == lane)
    return c[0] * cw + dot(cb, p2), q2


def rolled(x):
    return pltpu.roll(x, 64, axis=1)


def packed(x):
    lane = iota((BLK // 2, 128), 1)
    low, high = x[: BLK // 2, :128], x[BLK // 2 :, :128]
    return jnp.concatenate([x[:, 128:], jnp.where(lane >= 64, low, rolled(high))], axis=0)


def unpacked(x):
    lane = iota((BLK // 2, 128), 1)
    shared = x[BLK:PACK]
    low = jnp.where(lane >= 64, shared, 0.0)
    high = jnp.where(lane >= 64, rolled(shared), 0.0)
    return jnp.concatenate([jnp.concatenate([low, high], axis=0), x[:BLK]], axis=1)


def sent_sum(gram, left_sq, right_sq):
    row = iota((SUM - PACK, 128), 0)
    side = jnp.zeros((SUM - PACK, 128), F32)
    for n, value in enumerate((left_sq[:, :128], left_sq[:, 128:], right_sq[:, :128], right_sq[:, 128:])):
        side = jnp.where(row == n, value, side)
    return jnp.concatenate([packed(gram), side], axis=0).astype(BF)


def step_of(total):
    row, lane = iota((BLK, 256), 0), iota((BLK, 256), 1)
    gram, n = unpacked(total), total[PACK:]
    left_sq = jnp.concatenate([n[0:1], n[1:2]], axis=1)
    right_sq = jnp.concatenate([n[2:3], n[3:4]], axis=1)
    left_sq = jnp.sum(jnp.where(lane == row, left_sq, 0.0), axis=1, keepdims=True)
    corr = jnp.where(lane >= 64, gram * lax.rsqrt(left_sq) * lax.rsqrt(right_sq), 0.0)
    square = jnp.sum(jnp.sum(corr * corr, axis=0, keepdims=True), axis=1, keepdims=True)
    return corr * (8.0 * lax.rsqrt(2.0 * square + 1e-12))


def keep_left(ref, q1, nkt):
    for rows_of, value in ((pl.ds(0, BLK), q1), (pl.ds(BLK, BLK), nkt)):
        ref[0, rows_of] = value.astype(BF)
        ref[1, rows_of, :128] = value[:, :128].astype(BF)
        ref[1, rows_of, 128:] = rolled(value[:, 128:]).astype(BF)


def keep_right(ref, k, q2):
    for rows_of, value in ((pl.ds(0, BLK), k), (pl.ds(BLK, BLK), q2)):
        ref[0, rows_of] = value.astype(BF)
        ref[1, rows_of, :128] = rolled(value[:, :128]).astype(BF)
        ref[1, rows_of, 128:] = value[:, 128:].astype(BF)


def kernel(
    nx, ny, npos,
    w_hbm, out_v,
    w, own_l, own_r, in_l, in_r, far_l, far_r, raw_l, raw_r,
    ql, qr, pql, nqr, wl, wr, acc, part, got, c_own, c_prev, c_next,
    load_sem, sum_send, sum_recv, mv_send, mv_recv, c_send, c_recv, raw_send, raw_recv,
):
    r, p = lax.axis_index("rows"), lax.axis_index("pairs")
    x, y = lax.rem(r, nx), lax.div(r, nx)
    nxt, prv = lax.rem(p + 1, npos), lax.rem(p + npos - 1, npos)
    rows = w_hbm.shape[0]
    ch = rows // CHUNKS
    g = ch // 2

    def along(axis, k):
        if axis == 0:
            return (y * nx + lax.rem(x + k, nx), p)
        return (lax.rem(y + k, ny) * nx + x, p)

    ring = (nx, ny)
    peers = [along(a, k) for a in (0, 1) for k in range(1, ring[a])] + [(r, nxt), (r, prv)]

    loads = [
        pltpu.make_async_copy(
            w_hbm.at[pl.ds(c * ch, ch)], w.at[pl.ds(c * ch, ch)], load_sem.at[c]
        )
        for c in range(CHUNKS)
    ]
    for copy in loads:
        copy.start()
    barrier = pltpu.get_barrier_semaphore()
    for peer in peers:
        pl.semaphore_signal(barrier, inc=1, device_id=peer, device_id_type=MESH)

    started = []

    def remote(src, dst, send, recv, target):
        copy = pltpu.make_async_remote_copy(
            src_ref=src, dst_ref=dst, send_sem=send, recv_sem=recv,
            device_id=target, device_id_type=MESH,
        )
        copy.start()
        started.append(copy)
        return copy

    flight = {}

    def send_piece(rnd, phase, n):
        first, start, size = PIECES[n]
        axis = (phase + first) % 2
        rows_of = pl.ds(start, size)
        flight[rnd, phase, n] = [
            remote(
                part.at[rnd, phase, rows_of], got.at[rnd, phase, k - 1, rows_of],
                sum_send.at[rnd, phase, n, k - 1], sum_recv.at[rnd, phase, n, k - 1],
                along(axis, k),
            )
            for k in (2, 1, 3) if k < ring[axis]
        ]

    def collect(rnd, phase, n):
        first, start, size = PIECES[n]
        rows_of = pl.ds(start, size)
        for copy in flight[rnd, phase, n]:
            copy.wait_recv()
        total = part[rnd, phase, rows_of].astype(F32)
        for k in range(ring[(phase + first) % 2] - 1):
            total = total + got[rnd, phase, k, rows_of].astype(F32)
        return total

    def start_sum(rnd, payload):
        part[rnd, 0] = payload
        for n in ORDER:
            send_piece(rnd, 0, n)

    def end_sum(rnd):
        for n in ORDER:
            part[rnd, 1, pl.ds(PIECES[n][1], PIECES[n][2])] = collect(rnd, 0, n).astype(BF)
            send_piece(rnd, 1, n)
        totals = {n: collect(rnd, 1, n) for n in ORDER}
        return jnp.concatenate([totals[n] for n in range(len(PIECES))], axis=0)

    def exchange(rnd, c):
        c_own[rnd] = packed(c).astype(BF)
        return (
            remote(c_own.at[rnd], c_prev.at[rnd], c_send.at[rnd, 0], c_recv.at[rnd, 0], (r, nxt)),
            remote(c_own.at[rnd], c_next.at[rnd], c_send.at[rnd, 1], c_recv.at[rnd, 1], (r, prv)),
        )

    def turn_left(c, src, weights, dst):
        a = dot(src[pl.ds(c * ch, g)], weights[0])
        b = dot(src[pl.ds(c * ch + g, g)], weights[1])
        dst[c, :g] = a[:, :128].astype(BF)
        dst[c, g : 2 * g] = b[:, :128].astype(BF)
        dst[c, 2 * g :] = (a[:, 128:] + b[:, 128:]).astype(BF)

    def turn_right(c, src, weights, dst):
        a = dot(src[pl.ds(c * ch, g)], weights[0])
        b = dot(src[pl.ds(c * ch + g, g)], weights[1])
        dst[c, :g] = a[:, 128:].astype(BF)
        dst[c, g : 2 * g] = b[:, 128:].astype(BF)
        dst[c, 2 * g :] = (a[:, :128] + b[:, :128]).astype(BF)

    acc[0] = jnp.zeros((256, 256), F32)
    sq = jnp.zeros((8, WIDE), F32)
    raw = None
    for c in range(CHUNKS):
        loads[c].wait()
        if c == PRE:
            pl.semaphore_wait(barrier, len(peers))
            early = pl.ds(0, PRE * ch)
            raw = (
                remote(w.at[early], raw_l, raw_send.at[0], raw_recv.at[0], (r, nxt)),
                remote(w.at[early], raw_r, raw_send.at[1], raw_recv.at[1], (r, prv)),
            )
        block = w[pl.ds(c * ch, ch)]
        acc[0] += dot_tn(block[:, :256], block[:, 128:])
        wide = block.astype(F32)
        sq = sq + jnp.sum((wide * wide).reshape(ch // 8, 8, WIDE), axis=0)
    sq = jnp.sum(sq, axis=0, keepdims=True)
    start_sum(0, sent_sum(acc[0, :BLK], sq[:, :256], sq[:, 128:]))
    step = step_of(end_sum(0))
    up, down = exchange(0, step)
    keep_left(ql, *left_columns(step))
    keep_right(qr, *right_columns(step))

    first = {}
    for c in range(PRE, CHUNKS):
        turn_left(c, w, ql, own_l)
        turn_right(c, w, qr, own_r)
        first[c] = (
            remote(own_l.at[c], in_l.at[c], mv_send.at[0, c], mv_recv.at[0, c], (r, nxt)),
            remote(own_r.at[c], in_r.at[c], mv_send.at[1, c], mv_recv.at[1, c], (r, prv)),
        )
    up.wait_recv()
    down.wait_recv()
    keep_left(pql, *left_columns(unpacked(c_prev[0].astype(F32))))
    keep_right(nqr, *right_columns(unpacked(c_next[0].astype(F32))))

    acc[0] = jnp.zeros((256, 256), F32)
    acc[1] = jnp.zeros((256, 256), F32)
    sq_l = [jnp.zeros((8, 128), F32), jnp.zeros((8, 128), F32)]
    sq_r = [jnp.zeros((8, 128), F32), jnp.zeros((8, 128), F32)]
    second = []

    def squares(total, block):
        wide = block.astype(F32)
        wide = wide * wide
        a = jnp.sum(wide[: 2 * g].reshape(2 * g // 8, 8, 128), axis=0)
        b = jnp.sum(wide[2 * g :].reshape(g // 8, 8, 128), axis=0)
        return [total[0] + a, total[1] + b]

    for c in range(CHUNKS):
        if c == 0:
            raw[0].wait_recv()
            raw[1].wait_recv()
        if c < PRE:
            turn_left(c, raw_l, pql, in_l)
            turn_right(c, raw_r, nqr, in_r)
        else:
            first[c][0].wait_recv()
            first[c][1].wait_recv()
        second.append((
            remote(in_l.at[c], far_l.at[c], mv_send.at[2, c], mv_recv.at[2, c], (r, nxt)),
            remote(in_r.at[c], far_r.at[c], mv_send.at[3, c], mv_recv.at[3, c], (r, prv)),
        ))
        left, right = in_l[c], in_r[c]
        lb, rb = left[2 * g :], right[2 * g :]
        for half in range(2):
            a = jnp.concatenate([left[half * g : half * g + g], lb], axis=1)
            b = jnp.concatenate([rb, right[half * g : half * g + g]], axis=1)
            acc[half] += dot_tn(a, b)
        sq_l = squares(sq_l, left)
        sq_r = squares(sq_r, right)

    def folded(total):
        a, b = (jnp.sum(v, axis=0, keepdims=True) for v in total)
        return a, b + rolled(b)

    la, lb = folded(sq_l)
    ra, rb = folded(sq_r)
    lower = jnp.concatenate([acc[1, :128], acc[1, BLK:]], axis=0)
    lower = jnp.concatenate([rolled(lower[:, :128]), lower[:, 128:]], axis=1)
    start_sum(1, sent_sum(
        acc[0, :BLK] + lower,
        jnp.concatenate([la, lb], axis=1),
        jnp.concatenate([rb, ra], axis=1),
    ))
    for c in range(PRE):
        turn_left(c, w, ql, own_l)
        turn_right(c, w, qr, own_r)
    up, down = exchange(1, step_of(end_sum(1)))
    up.wait_recv()
    down.wait_recv()
    q1, nkt = left_columns(unpacked(c_prev[1].astype(F32)))
    k, q2 = right_columns(unpacked(c_next[1].astype(F32)))
    none = jnp.zeros((64, 256), BF)
    for ref, top, low in ((wl, q1, nkt), (wr, k, q2)):
        top, low = top.astype(BF), low.astype(BF)
        ref[0, :BLK] = top
        ref[0, BLK:256] = none
        ref[1, :128] = top[:128]
        ref[1, 128:192] = none
        ref[1, 192:256] = top[128:]
        ref[0, 256:320] = none
        ref[0, 320:] = low
        ref[1, 256:320] = low[:64]
        ref[1, 320:384] = none
        ref[1, 384:] = low[64:]

    for c in range(0, CHUNKS, 2):
        for n in (c, c + 1):
            second[n][0].wait_recv()
            second[n][1].wait_recv()
        for half in range(2):
            a_of, b_of = pl.ds(half * g, g), pl.ds(2 * g, g)
            to_left = jnp.concatenate([
                jnp.concatenate([far_l[n, a_of], far_l[n, b_of], own_r[n, b_of], own_r[n, a_of]], axis=1)
                for n in (c, c + 1)
            ], axis=0)
            to_right = jnp.concatenate([
                jnp.concatenate([own_l[n, a_of], own_l[n, b_of], far_r[n, b_of], far_r[n, a_of]], axis=1)
                for n in (c, c + 1)
            ], axis=0)
            a, b = dot(to_left, wl[half]), dot(to_right, wr[half])
            for n in range(2):
                rows_of = pl.ds((c + n) * ch + half * g, g)
                an, bn = a[n * g : n * g + g], b[n * g : n * g + g]
                out_v[rows_of, :128] = an[:, :128].astype(BF)
                out_v[rows_of, 128:256] = (an[:, 128:] + bn[:, :128]).astype(BF)
                out_v[rows_of, 256:] = bn[:, 128:].astype(BF)
    for copy in started:
        copy.wait_send()


def local(nx, ny, npos, latent):
    rows = latent.shape[0]
    g = rows // CHUNKS // 2
    block = pltpu.VMEM((CHUNKS, 3 * g, 128), BF)
    return pl.pallas_call(
        functools.partial(kernel, nx, ny, npos),
        out_shape=jax.ShapeDtypeStruct(latent.shape, BF),
        in_specs=[pl.BlockSpec(memory_space=pltpu.HBM)],
        out_specs=pl.BlockSpec(memory_space=pltpu.VMEM),
        scratch_shapes=[
            pltpu.VMEM((rows, WIDE), BF),
            block, block, block, block, block, block,
            pltpu.VMEM((PRE * 2 * g, WIDE), BF),
            pltpu.VMEM((PRE * 2 * g, WIDE), BF),
            pltpu.VMEM((2, WIDE, 256), BF),
            pltpu.VMEM((2, WIDE, 256), BF),
            pltpu.VMEM((2, WIDE, 256), BF),
            pltpu.VMEM((2, WIDE, 256), BF),
            pltpu.VMEM((2, 512, 256), BF),
            pltpu.VMEM((2, 512, 256), BF),
            pltpu.VMEM((2, 256, 256), F32),
            pltpu.VMEM((2, 2, SUM, 128), BF),
            pltpu.VMEM((2, 2, max(nx, ny) - 1, SUM, 128), BF),
            pltpu.VMEM((2, PACK, 128), BF),
            pltpu.VMEM((2, PACK, 128), BF),
            pltpu.VMEM((2, PACK, 128), BF),
            pltpu.SemaphoreType.DMA((CHUNKS,)),
            pltpu.SemaphoreType.DMA((2, 2, len(PIECES), max(nx, ny) - 1)),
            pltpu.SemaphoreType.DMA((2, 2, len(PIECES), max(nx, ny) - 1)),
            pltpu.SemaphoreType.DMA((4, CHUNKS)),
            pltpu.SemaphoreType.DMA((4, CHUNKS)),
            pltpu.SemaphoreType.DMA((2, 2)),
            pltpu.SemaphoreType.DMA((2, 2)),
            pltpu.SemaphoreType.DMA((2,)),
            pltpu.SemaphoreType.DMA((2,)),
        ],
        compiler_params=pltpu.CompilerParams(
            collective_id=0, has_side_effects=True, vmem_limit_bytes=54_000_000
        ),
    )(latent)


def solution(mesh):
    side = math.isqrt(mesh.shape["rows"])
    return jax.shard_map(
        functools.partial(local, side, mesh.shape["rows"] // side, mesh.shape["pairs"]),
        mesh=mesh,
        in_specs=(P("rows", "pairs"),),
        out_specs=P("rows", "pairs"),
        check_vma=False,
    )
```

time: 54.1 us -> 41.7 us (0.77)
  the two profiles are of different devices: /device:TPU:97 before, /device:TPU:1 now
where the time goes in v2:
time: 41.7 us; the launch traced here: 41.2 us
  Pallas kernels  40.1 us (96%)
  local copies, waits for them, and re-layouts  1.15 us (3%)
    pallas_call x1, Pallas kernels, local(): pl.pallas_call(functools.partial(kernel, nx, ny, npos), out_shape=jax.Sha...  40.1 us
    unnamed x1, local copies, waits for them, and re-layouts  1.15 us

profile of v2, /device:TPU:1, one launch (start us, length us, event | category | flops | bytes accessed | tf_op | source)
XLA Modules:
  0.0 41.2 jit_solution(2979303765412488481)
XLA Ops:
  0.0 40.1 %shard_map.17 = bf16[2048,384]{1,0:T(8,128)(2,1)S(1)} custom-call(bf16[2048,384]{1,0:T(8,128)(2,1)} %w_hbm.1), custom_call_target="tpu_custom_call" | custom-call | tf_op jit(solution)/shard_map/pallas_call | solution.py:373
  40.1 1.1 %copy.3 = bf16[2048,384]{1,0:T(8,128)(2,1)} copy(bf16[2048,384]{1,0:T(8,128)(2,1)S(1)} %shard_map.17) | data formatting | bytes 3145728

commit v3 on v2

v3 whole, which is shorter than its diff:
```python
import functools
import math

import jax
import jax.numpy as jnp
from jax import lax
from jax.experimental import pallas as pl
from jax.experimental.pallas import tpu as pltpu
from jax.sharding import PartitionSpec as P

BF = jnp.bfloat16
F32 = jnp.float32
BLK = 192
WIDE = 2 * BLK
CHUNKS = 8
PRE = 4
PACK = 288
SUM = 304
PIECES = ((0, 0, 144), (1, 144, 160))
LOADS = 4
MESH = pl.DeviceIdType.MESH


def polynomial():
    a = 1.5 / math.sqrt(65.0)
    t = a * a
    f = [2.25, -2.4375, 1.6875, -0.5625, 0.0625]
    c = []
    for k in range(5):
        c.append(a * sum(f[n] * math.comb(n, k) * t ** (n - k) for n in range(k, 5)))
    return t, c


def dot(a, b):
    return jnp.dot(a, b, preferred_element_type=F32)


def dot_nt(a, b):
    return lax.dot_general(a, b, (((1,), (1,)), ((), ())), preferred_element_type=F32)


def dot_tn(a, b):
    return lax.dot_general(a, b, (((0,), (0,)), ((), ())), preferred_element_type=F32)


def iota(shape, dim):
    return lax.broadcasted_iota(jnp.int32, shape, dim)


def series(h, c, full, eye):
    hb = h.astype(BF)
    h2 = dot(hb, full(hb))
    rest = c[1] * h + c[2] * h2 + dot(h2.astype(BF), full((c[3] * h + c[4] * h2).astype(BF)))
    return jnp.where(eye, rest + c[0], rest), full(rest.astype(BF))


def below(x):
    return jnp.concatenate([x, jnp.zeros((64, 256), x.dtype)], axis=0)


def above(x):
    return jnp.concatenate([jnp.zeros((64, 256), x.dtype), x], axis=0)


def scale_of(corr):
    square = jnp.sum(jnp.sum(corr * corr, axis=0, keepdims=True), axis=1, keepdims=True)
    return 8.0 * lax.rsqrt(2.0 * square + 1e-12)


def left_columns(corr, scale):
    t, c = polynomial()
    cb = corr.astype(BF)
    row, lane = iota((BLK, 256), 0), iota((BLK, 256), 1)
    ct = below(corr).T[64:]
    q1, p1 = series((t * scale * scale) * dot_nt(cb, below(cb)), c, below, row == lane)
    return q1, -scale * (c[0] * ct + dot(ct.astype(BF), p1))


def right_columns(corr, scale):
    t, c = polynomial()
    cb = corr.astype(BF)
    ctb = below(corr).T[64:].astype(BF)
    row, lane = iota((BLK, 256), 0), iota((BLK, 256), 1)
    q2, p2 = series((t * scale * scale) * dot_nt(ctb, above(ctb)), c, above, row + 64 == lane)
    return scale * (c[0] * corr + dot(cb, p2)), q2


def rolled(x):
    return pltpu.roll(x, 64, axis=1)


def packed(x):
    lane = iota((BLK // 2, 128), 1)
    low, high = x[: BLK // 2, :128], x[BLK // 2 :, :128]
    return jnp.concatenate([x[:, 128:], jnp.where(lane >= 64, low, rolled(high))], axis=0)


def unpacked(x):
    lane = iota((BLK // 2, 128), 1)
    shared = x[BLK:PACK]
    low = jnp.where(lane >= 64, shared, 0.0)
    high = jnp.where(lane >= 64, rolled(shared), 0.0)
    return jnp.concatenate([jnp.concatenate([low, high], axis=0), x[:BLK]], axis=1)


def sent_sum(gram, left_sq, right_sq):
    row = iota((SUM - PACK, 128), 0)
    side = jnp.zeros((SUM - PACK, 128), F32)
    for n, value in enumerate((left_sq[:, :128], left_sq[:, 128:], right_sq[:, :128], right_sq[:, 128:])):
        side = jnp.where(row == n, value, side)
    return jnp.concatenate([packed(gram), side], axis=0).astype(BF)


def corr_of(total):
    gram, n = unpacked(total), total[PACK:]
    row, lane = iota((BLK, 128), 0), iota((BLK, 128), 1)
    left_sq = jnp.where(row < 128, n[0:1], n[1:2])
    left_sq = jnp.where(lane == lax.rem(row, 128), left_sq, 0.0)
    left_sq = jnp.sum(left_sq, axis=1, keepdims=True)
    right_sq = jnp.concatenate([n[2:3], n[3:4]], axis=1)
    corr = gram * lax.rsqrt(left_sq) * lax.rsqrt(right_sq)
    return jnp.where(iota((BLK, 256), 1) >= 64, corr, 0.0)


def keep_left(ref, q1, nkt):
    for rows_of, value in ((pl.ds(0, BLK), q1), (pl.ds(BLK, BLK), nkt)):
        ref[0, rows_of] = value.astype(BF)
        ref[1, rows_of, :128] = value[:, :128].astype(BF)
        ref[1, rows_of, 128:] = rolled(value[:, 128:]).astype(BF)


def keep_right(ref, k, q2):
    for rows_of, value in ((pl.ds(0, BLK), k), (pl.ds(BLK, BLK), q2)):
        ref[0, rows_of] = value.astype(BF)
        ref[1, rows_of, :128] = rolled(value[:, :128]).astype(BF)
        ref[1, rows_of, 128:] = value[:, 128:].astype(BF)


def kernel(
    nx, ny, npos,
    w_hbm, out_v,
    w, own_l, own_r, in_l, in_r, far_l, far_r, raw_l, raw_r,
    ql, qr, pql, nqr, wl, acc, part, got, c_own, c_prev, c_next,
    load_sem, sum_send, sum_recv, mv_send, in_recv, far_recv, c_send, c_recv, raw_send, raw_recv,
):
    r, p = lax.axis_index("rows"), lax.axis_index("pairs")
    x, y = lax.rem(r, nx), lax.div(r, nx)
    nxt, prv = lax.rem(p + 1, npos), lax.rem(p + npos - 1, npos)
    rows = w_hbm.shape[0]
    ch = rows // CHUNKS
    g = ch // 2

    def along(axis, k):
        if axis == 0:
            return (y * nx + lax.rem(x + k, nx), p)
        return (lax.rem(y + k, ny) * nx + x, p)

    ring = (nx, ny)
    peers = [along(a, k) for a in (0, 1) for k in range(1, ring[a])] + [(r, nxt), (r, prv)]

    piece = rows // LOADS
    loads = [
        pltpu.make_async_copy(
            w_hbm.at[pl.ds(c * piece, piece)], w.at[pl.ds(c * piece, piece)], load_sem.at[c]
        )
        for c in range(LOADS)
    ]
    for copy in loads:
        copy.start()
    barrier = pltpu.get_barrier_semaphore()
    for peer in peers:
        pl.semaphore_signal(barrier, inc=1, device_id=peer, device_id_type=MESH)

    def remote(src, dst, send, recv, target):
        pltpu.make_async_remote_copy(
            src_ref=src, dst_ref=dst, send_sem=send, recv_sem=recv,
            device_id=target, device_id_type=MESH,
        ).start()

    def arrived(ref, sem):
        pltpu.make_async_copy(ref, ref, sem).wait()

    def pieces_of(phase, n):
        first, start, size = PIECES[n]
        axis = (phase + first) % 2
        return axis, pl.ds(start, size), pl.ds(0, ring[axis] - 1)

    def send_piece(rnd, phase, n):
        axis, rows_of, _ = pieces_of(phase, n)
        for k in (2, 1, 3):
            if k < ring[axis]:
                remote(
                    part.at[rnd, phase, rows_of], got.at[rnd, phase, k - 1, rows_of],
                    sum_send.at[rnd, phase, n], sum_recv.at[rnd, phase, n], along(axis, k),
                )

    def collect(rnd, phase, n):
        axis, rows_of, slots = pieces_of(phase, n)
        arrived(got.at[rnd, phase, slots, rows_of], sum_recv.at[rnd, phase, n])
        total = part[rnd, phase, rows_of].astype(F32)
        for k in range(ring[axis] - 1):
            total = total + got[rnd, phase, k, rows_of].astype(F32)
        return total

    def start_sum(rnd, payload):
        part[rnd, 0] = payload
        for n in range(2):
            send_piece(rnd, 0, n)

    def end_sum(rnd):
        for n in range(2):
            part[rnd, 1, pl.ds(PIECES[n][1], PIECES[n][2])] = collect(rnd, 0, n).astype(BF)
            send_piece(rnd, 1, n)
        return jnp.concatenate([collect(rnd, 1, n) for n in range(2)], axis=0)

    def sum_sent(rnd):
        for phase in range(2):
            for n in range(2):
                _, rows_of, slots = pieces_of(phase, n)
                arrived(got.at[rnd, phase, slots, rows_of], sum_send.at[rnd, phase, n])

    def exchange(rnd, corr):
        c_own[rnd] = packed(corr).astype(BF)
        remote(c_own.at[rnd], c_prev.at[rnd], c_send.at[rnd], c_recv.at[rnd, 0], (r, nxt))
        remote(c_own.at[rnd], c_next.at[rnd], c_send.at[rnd], c_recv.at[rnd, 1], (r, prv))

    def turn_left(c, src, weights, dst):
        a = dot(src[pl.ds(c * ch, g)], weights[0])
        b = dot(src[pl.ds(c * ch + g, g)], weights[1])
        dst[c, :g] = a[:, :128].astype(BF)
        dst[c, g : 2 * g] = b[:, :128].astype(BF)
        dst[c, 2 * g :] = (a[:, 128:] + b[:, 128:]).astype(BF)

    def turn_right(c, src, weights, dst):
        a = dot(src[pl.ds(c * ch, g)], weights[0])
        b = dot(src[pl.ds(c * ch + g, g)], weights[1])
        dst[c, :g] = a[:, 128:].astype(BF)
        dst[c, g : 2 * g] = b[:, 128:].astype(BF)
        dst[c, 2 * g :] = (a[:, :128] + b[:, :128]).astype(BF)

    early = pl.ds(0, PRE * ch)
    for c in range(PRE * ch // piece):
        loads[c].wait()
    pl.semaphore_wait(barrier, len(peers))
    remote(w.at[early], raw_l, raw_send, raw_recv.at[0], (r, nxt))
    remote(w.at[early], raw_r, raw_send, raw_recv.at[1], (r, prv))

    sq = jnp.zeros((8, WIDE), F32)
    for c in range(LOADS):
        if c * piece >= PRE * ch:
            loads[c].wait()
        block = w[pl.ds(c * piece, piece)]
        new = dot_tn(block[:, :256], block[:, 128:])[:BLK]
        if c == 0:
            acc[...] = new
        else:
            acc[...] += new
        wide = block.astype(F32)
        sq = sq + jnp.sum((wide * wide).reshape(piece // 8, 8, WIDE), axis=0)
    sq = jnp.sum(sq, axis=0, keepdims=True)
    start_sum(0, sent_sum(acc[...], sq[:, :256], sq[:, 128:]))
    corr = corr_of(end_sum(0))
    exchange(0, corr)
    scale = scale_of(corr)
    keep_left(ql, *left_columns(corr, scale))
    keep_right(qr, *right_columns(corr, scale))

    for c in range(PRE, CHUNKS):
        turn_left(c, w, ql, own_l)
        remote(own_l.at[c], in_l.at[c], mv_send.at[0], in_recv.at[0, c - PRE], (r, nxt))
        turn_right(c, w, qr, own_r)
        remote(own_r.at[c], in_r.at[c], mv_send.at[1], in_recv.at[1, c - PRE], (r, prv))
    arrived(c_prev.at[0], c_recv.at[0, 0])
    arrived(c_next.at[0], c_recv.at[0, 1])
    corr = unpacked(c_prev[0].astype(F32))
    keep_left(pql, *left_columns(corr, scale_of(corr)))
    corr = unpacked(c_next[0].astype(F32))
    keep_right(nqr, *right_columns(corr, scale_of(corr)))

    sq_l = [jnp.zeros((8, 128), F32), jnp.zeros((8, 128), F32)]
    sq_r = [jnp.zeros((8, 128), F32), jnp.zeros((8, 128), F32)]

    def squares(total, block):
        wide = block.astype(F32)
        wide = wide * wide
        a = jnp.sum(wide[: 2 * g].reshape(2 * g // 8, 8, 128), axis=0)
        b = jnp.sum(wide[2 * g :].reshape(g // 8, 8, 128), axis=0)
        return [total[0] + a, total[1] + b]

    for c in range(CHUNKS):
        if c == 0:
            arrived(raw_l, raw_recv.at[0])
            arrived(raw_r, raw_recv.at[1])
        if c < PRE:
            turn_left(c, raw_l, pql, in_l)
            turn_right(c, raw_r, nqr, in_r)
        else:
            arrived(in_l.at[c], in_recv.at[0, c - PRE])
            arrived(in_r.at[c], in_recv.at[1, c - PRE])
        remote(in_l.at[c], far_l.at[c], mv_send.at[2], far_recv.at[0], (r, nxt))
        remote(in_r.at[c], far_r.at[c], mv_send.at[3], far_recv.at[1], (r, prv))
        left, right = in_l[c], in_r[c]
        lb, rb = left[2 * g :], right[2 * g :]
        a = jnp.concatenate([left[: 2 * g], jnp.concatenate([lb, rolled(lb)], axis=0)], axis=1)
        b = jnp.concatenate([jnp.concatenate([rb, rolled(rb)], axis=0), right[: 2 * g]], axis=1)
        new = dot_tn(a, b)[:BLK]
        if c == 0:
            acc[...] = new
        else:
            acc[...] += new
        sq_l = squares(sq_l, left)
        sq_r = squares(sq_r, right)

    def folded(total):
        a, b = (jnp.sum(v, axis=0, keepdims=True) for v in total)
        return a, b + rolled(b)

    la, lb = folded(sq_l)
    ra, rb = folded(sq_r)
    start_sum(1, sent_sum(
        acc[...], jnp.concatenate([la, lb], axis=1), jnp.concatenate([rb, ra], axis=1)
    ))
    for c in range(PRE):
        turn_left(c, w, ql, own_l)
        turn_right(c, w, qr, own_r)
    sum_sent(0)
    for side in range(2):
        arrived((own_l, own_r)[side].at[pl.ds(PRE, CHUNKS - PRE)], mv_send.at[side])
    arrived(w.at[pl.ds(0, 2 * PRE * ch)], raw_send)
    arrived(c_prev, c_send.at[0])
    exchange(1, corr_of(end_sum(1)))

    none = jnp.zeros((64, 256), BF)

    def keep_last(ref, top, low):
        top, low = top.astype(BF), low.astype(BF)
        ref[0, :BLK] = top
        ref[0, BLK:256] = none
        ref[1, :128] = top[:128]
        ref[1, 128:192] = none
        ref[1, 192:256] = top[128:]
        ref[0, 256:320] = none
        ref[0, 320:] = low
        ref[1, 256:320] = low[:64]
        ref[1, 320:384] = none
        ref[1, 384:] = low[64:]

    def finish(side, first):
        from_l, from_r = ((far_l, own_r), (own_l, far_r))[side]
        arrived((c_prev, c_next)[side].at[1], c_recv.at[1, side])
        corr = unpacked((c_prev, c_next)[side][1].astype(F32))
        keep_last(wl, *(left_columns, right_columns)[side](corr, scale_of(corr)))
        arrived((far_l, far_r)[side], far_recv.at[side])
        outer = (pl.ds(0, 128), pl.ds(256, 128))[side]
        for c in range(0, CHUNKS, 4):
            for half in range(2):
                a_of, b_of = pl.ds(half * g, g), pl.ds(2 * g, g)
                terms = jnp.concatenate([
                    jnp.concatenate(
                        [from_l[n, a_of], from_l[n, b_of], from_r[n, b_of], from_r[n, a_of]], axis=1
                    )
                    for n in range(c, c + 4)
                ], axis=0)
                a = dot(terms, wl[half])
                for n in range(4):
                    rows_of = pl.ds((c + n) * ch + half * g, g)
                    pair = a[n * g : n * g + g, :128], a[n * g : n * g + g, 128:]
                    out_v[rows_of, outer] = pair[side].astype(BF)
                    middle = pair[1 - side]
                    if not first:
                        middle = middle + out_v[rows_of, 128:256].astype(F32)
                    out_v[rows_of, 128:256] = middle.astype(BF)

    @pl.when(lax.rem(p, 2) == 0)
    def _():
        finish(1, True)
        finish(0, False)

    @pl.when(lax.rem(p, 2) == 1)
    def _():
        finish(0, True)
        finish(1, False)

    sum_sent(1)
    arrived(in_l, mv_send.at[2])
    arrived(in_r, mv_send.at[3])
    arrived(c_prev, c_send.at[1])


def local(nx, ny, npos, latent):
    rows = latent.shape[0]
    g = rows // CHUNKS // 2
    block = pltpu.VMEM((CHUNKS, 3 * g, 128), BF)
    return pl.pallas_call(
        functools.partial(kernel, nx, ny, npos),
        out_shape=jax.ShapeDtypeStruct(latent.shape, BF),
        in_specs=[pl.BlockSpec(memory_space=pltpu.HBM)],
        out_specs=pl.BlockSpec(memory_space=pltpu.VMEM),
        scratch_shapes=[
            pltpu.VMEM((rows, WIDE), BF),
            block, block, block, block, block, block,
            pltpu.VMEM((PRE * 2 * g, WIDE), BF),
            pltpu.VMEM((PRE * 2 * g, WIDE), BF),
            pltpu.VMEM((2, WIDE, 256), BF),
            pltpu.VMEM((2, WIDE, 256), BF),
            pltpu.VMEM((2, WIDE, 256), BF),
            pltpu.VMEM((2, WIDE, 256), BF),
            pltpu.VMEM((2, 512, 256), BF),
            pltpu.VMEM((BLK, 256), F32),
            pltpu.VMEM((2, 2, SUM, 128), BF),
            pltpu.VMEM((2, 2, max(nx, ny) - 1, SUM, 128), BF),
            pltpu.VMEM((2, PACK, 128), BF),
            pltpu.VMEM((2, PACK, 128), BF),
            pltpu.VMEM((2, PACK, 128), BF),
            pltpu.SemaphoreType.DMA((LOADS,)),
            pltpu.SemaphoreType.DMA((2, 2, len(PIECES))),
            pltpu.SemaphoreType.DMA((2, 2, len(PIECES))),
            pltpu.SemaphoreType.DMA((4,)),
            pltpu.SemaphoreType.DMA((2, CHUNKS - PRE)),
            pltpu.SemaphoreType.DMA((2,)),
            pltpu.SemaphoreType.DMA((2,)),
            pltpu.SemaphoreType.DMA((2, 2)),
            pltpu.SemaphoreType.DMA,
            pltpu.SemaphoreType.DMA((2,)),
        ],
        compiler_params=pltpu.CompilerParams(
            collective_id=0, has_side_effects=True, vmem_limit_bytes=54_000_000
        ),
    )(latent)


def solution(mesh):
    side = math.isqrt(mesh.shape["rows"])
    return jax.shard_map(
        functools.partial(local, side, mesh.shape["rows"] // side, mesh.shape["pairs"]),
        mesh=mesh,
        in_specs=(P("rows", "pairs"),),
        out_specs=P("rows", "pairs"),
        check_vma=False,
    )
```

time: 41.7 us -> 39.6 us (0.950)
  Pallas kernels: 40.1 us -> 38.4 us
    pallas_call x1, Pallas kernels: 40.1 us -> 38.4 us  [local(): pl.pallas_call(functools.partial(kernel, nx, ny, npos), out_shape=jax.Sha...]
where the time goes in v3:
time: 39.6 us; the launch traced here: 39.5 us
  Pallas kernels  38.4 us (97%)
  local copies, waits for them, and re-layouts  1.15 us (3%)
    pallas_call x1, Pallas kernels, local(): pl.pallas_call(functools.partial(kernel, nx, ny, npos), out_shape=jax.Sha...  38.4 us
    unnamed x1, local copies, waits for them, and re-layouts  1.15 us

profile of v3, /device:TPU:1, one launch (start us, length us, event | category | flops | bytes accessed | tf_op | source)
XLA Modules:
  0.0 39.5 jit_solution(82287408684812332)
XLA Ops:
  0.0 38.4 %shard_map.17 = bf16[2048,384]{1,0:T(8,128)(2,1)S(1)} custom-call(bf16[2048,384]{1,0:T(8,128)(2,1)} %w_hbm.1), custom_call_target="tpu_custom_call" | custom-call | tf_op jit(solution)/shard_map/pallas_call | solution.py:394
  38.4 1.1 %copy.3 = bf16[2048,384]{1,0:T(8,128)(2,1)} copy(bf16[2048,384]{1,0:T(8,128)(2,1)S(1)} %shard_map.17) | data formatting | bytes 3145728

commit v4 on v3

--- a/solution.py
+++ b/solution.py
@@ -18,6 +18,8 @@
 SUM = 304
 PIECES = ((0, 0, 144), (1, 144, 160))
 LOADS = 4
+TILE = 16
+LATE = 2
 MESH = pl.DeviceIdType.MESH
 
 
@@ -140,8 +142,10 @@
     nx, ny, npos,
     w_hbm, out_v,
     w, own_l, own_r, in_l, in_r, far_l, far_r, raw_l, raw_r,
-    ql, qr, pql, nqr, wl, acc, part, got, c_own, c_prev, c_next,
+    ql, qr, pql, nqr, wl, acc, part, got, c_own, c_both,
+    tile_got, rest_got, sums, tot_prev, tot_next,
     load_sem, sum_send, sum_recv, mv_send, in_recv, far_recv, c_send, c_recv, raw_send, raw_recv,
+    tile_send, tile_recv, rest_send, rest_recv, spread_send, tot_recv,
 ):
     r, p = lax.axis_index("rows"), lax.axis_index("pairs")
     x, y = lax.rem(r, nx), lax.div(r, nx)
@@ -156,6 +160,7 @@
         return (lax.rem(y + k, ny) * nx + x, p)
 
     ring = (nx, ny)
+    c_prev, c_next = c_both.at[0], c_both.at[1]
     peers = [along(a, k) for a in (0, 1) for k in range(1, ring[a])] + [(r, nxt), (r, prv)]
 
     piece = rows // LOADS
@@ -185,44 +190,116 @@
         axis = (phase + first) % 2
         return axis, pl.ds(start, size), pl.ds(0, ring[axis] - 1)
 
-    def send_piece(rnd, phase, n):
+    def send_piece(phase, n):
         axis, rows_of, _ = pieces_of(phase, n)
         for k in (2, 1, 3):
             if k < ring[axis]:
                 remote(
-                    part.at[rnd, phase, rows_of], got.at[rnd, phase, k - 1, rows_of],
-                    sum_send.at[rnd, phase, n], sum_recv.at[rnd, phase, n], along(axis, k),
+                    part.at[0, phase, rows_of], got.at[phase, k - 1, rows_of],
+                    sum_send.at[phase, n], sum_recv.at[phase, n], along(axis, k),
                 )
 
-    def collect(rnd, phase, n):
+    def collect(phase, n):
         axis, rows_of, slots = pieces_of(phase, n)
-        arrived(got.at[rnd, phase, slots, rows_of], sum_recv.at[rnd, phase, n])
-        total = part[rnd, phase, rows_of].astype(F32)
+        arrived(got.at[phase, slots, rows_of], sum_recv.at[phase, n])
+        total = part[0, phase, rows_of].astype(F32)
         for k in range(ring[axis] - 1):
-            total = total + got[rnd, phase, k, rows_of].astype(F32)
+            total = total + got[phase, k, rows_of].astype(F32)
         return total
 
-    def start_sum(rnd, payload):
-        part[rnd, 0] = payload
+    def start_sum(payload):
+        part[0, 0] = payload
         for n in range(2):
-            send_piece(rnd, 0, n)
-
-    def end_sum(rnd):
+            send_piece(0, n)
+
+    def end_sum():
         for n in range(2):
-            part[rnd, 1, pl.ds(PIECES[n][1], PIECES[n][2])] = collect(rnd, 0, n).astype(BF)
-            send_piece(rnd, 1, n)
-        return jnp.concatenate([collect(rnd, 1, n) for n in range(2)], axis=0)
-
-    def sum_sent(rnd):
+            part[0, 1, pl.ds(PIECES[n][1], PIECES[n][2])] = collect(0, n).astype(BF)
+            send_piece(1, n)
+        return jnp.concatenate([collect(1, n) for n in range(2)], axis=0)
+
+    def sum_sent():
         for phase in range(2):
             for n in range(2):
                 _, rows_of, slots = pieces_of(phase, n)
-                arrived(got.at[rnd, phase, slots, rows_of], sum_send.at[rnd, phase, n])
-
-    def exchange(rnd, corr):
-        c_own[rnd] = packed(corr).astype(BF)
-        remote(c_own.at[rnd], c_prev.at[rnd], c_send.at[rnd], c_recv.at[rnd, 0], (r, nxt))
-        remote(c_own.at[rnd], c_next.at[rnd], c_send.at[rnd], c_recv.at[rnd, 1], (r, prv))
+                arrived(got.at[phase, slots, rows_of], sum_send.at[phase, n])
+
+    def exchange(corr):
+        c_own[...] = packed(corr).astype(BF)
+        remote(c_own, c_prev, c_send, c_recv.at[0], (r, nxt))
+        remote(c_own, c_next, c_send, c_recv.at[1], (r, prv))
+
+    plane = nx * ny
+    slots, rest = divmod(SUM // TILE, plane)
+    final = part.at[1, 0]
+    peer_at = [lax.rem(r + k, plane) for k in range(plane)]
+
+    def tile(n):
+        return pl.ds(n * TILE if isinstance(n, int) else pl.multiple_of(n * TILE, TILE), TILE)
+
+    def scatter(payload):
+        part[1, 0] = payload
+        for j in range(rest):
+            n = slots * plane + j
+
+            @pl.when(r != j)
+            def _():
+                remote(
+                    final.at[tile(n)], rest_got.at[lax.rem(r - j + plane, plane) - 1],
+                    rest_send.at[j], rest_recv, (j, p),
+                )
+
+        for s in range(slots):
+            for k in range(1, plane):
+                remote(
+                    final.at[tile(s * plane + peer_at[k])], tile_got.at[s, k - 1],
+                    tile_send, tile_recv, (peer_at[k], p),
+                )
+
+    def gather():
+        def spread(src, n, send):
+            for k in range(plane):
+                remote(src, tot_prev.at[tile(n)], send.at[0], tot_recv.at[0], (peer_at[k], nxt))
+                remote(src, tot_next.at[tile(n)], send.at[1], tot_recv.at[1], (peer_at[k], prv))
+
+        arrived(tile_got, tile_recv)
+        for s in range(slots):
+            n = s * plane + r
+            total = part[1, 0, tile(n)].astype(F32)
+            for k in range(plane - 1):
+                total = total + tile_got[s, k].astype(F32)
+            sums[s] = total.astype(BF)
+            spread(sums.at[s], n, spread_send.at[s])
+
+        @pl.when(r < rest)
+        def _():
+            n = slots * plane + r
+            arrived(rest_got, rest_recv)
+            total = part[1, 0, tile(n)].astype(F32)
+            for k in range(plane - 1):
+                total = total + rest_got[k].astype(F32)
+            sums[slots] = total.astype(BF)
+            spread(sums.at[slots], n, spread_send.at[slots])
+
+    def gathered():
+        everyone = pl.ds(0, plane * TILE)
+        for j in range(rest):
+            @pl.when(r != j)
+            def _():
+                arrived(final.at[tile(slots * plane + j)], rest_send.at[j])
+        arrived(tile_got, tile_send)
+        for s in range(slots):
+            for side in range(2):
+                arrived(tot_prev.at[everyone], spread_send.at[s, side])
+
+        @pl.when(r < rest)
+        def _():
+            for side in range(2):
+                arrived(tot_prev.at[everyone], spread_send.at[slots, side])
+
+    def forward(c):
+        remote(in_l.at[c], far_l.at[c], mv_send.at[2], far_recv.at[0], (r, nxt))
+        remote(in_r.at[c], far_r.at[c], mv_send.at[3], far_recv.at[1], (r, prv))
 
     def turn_left(c, src, weights, dst):
         a = dot(src[pl.ds(c * ch, g)], weights[0])
@@ -258,9 +335,9 @@
         wide = block.astype(F32)
         sq = sq + jnp.sum((wide * wide).reshape(piece // 8, 8, WIDE), axis=0)
     sq = jnp.sum(sq, axis=0, keepdims=True)
-    start_sum(0, sent_sum(acc[...], sq[:, :256], sq[:, 128:]))
-    corr = corr_of(end_sum(0))
-    exchange(0, corr)
+    start_sum(sent_sum(acc[...], sq[:, :256], sq[:, 128:]))
+    corr = corr_of(end_sum())
+    exchange(corr)
     scale = scale_of(corr)
     keep_left(ql, *left_columns(corr, scale))
     keep_right(qr, *right_columns(corr, scale))
@@ -270,11 +347,11 @@
         remote(own_l.at[c], in_l.at[c], mv_send.at[0], in_recv.at[0, c - PRE], (r, nxt))
         turn_right(c, w, qr, own_r)
         remote(own_r.at[c], in_r.at[c], mv_send.at[1], in_recv.at[1, c - PRE], (r, prv))
-    arrived(c_prev.at[0], c_recv.at[0, 0])
-    arrived(c_next.at[0], c_recv.at[0, 1])
-    corr = unpacked(c_prev[0].astype(F32))
+    arrived(c_prev, c_recv.at[0])
+    arrived(c_next, c_recv.at[1])
+    corr = unpacked(c_prev[...].astype(F32))
     keep_left(pql, *left_columns(corr, scale_of(corr)))
-    corr = unpacked(c_next[0].astype(F32))
+    corr = unpacked(c_next[...].astype(F32))
     keep_right(nqr, *right_columns(corr, scale_of(corr)))
 
     sq_l = [jnp.zeros((8, 128), F32), jnp.zeros((8, 128), F32)]
@@ -297,8 +374,8 @@
         else:
             arrived(in_l.at[c], in_recv.at[0, c - PRE])
             arrived(in_r.at[c], in_recv.at[1, c - PRE])
-        remote(in_l.at[c], far_l.at[c], mv_send.at[2], far_recv.at[0], (r, nxt))
-        remote(in_r.at[c], far_r.at[c], mv_send.at[3], far_recv.at[1], (r, prv))
+        if c < CHUNKS - LATE:
+            forward(c)
         left, right = in_l[c], in_r[c]
         lb, rb = left[2 * g :], right[2 * g :]
         a = jnp.concatenate([left[: 2 * g], jnp.concatenate([lb, rolled(lb)], axis=0)], axis=1)
@@ -317,18 +394,20 @@
 
     la, lb = folded(sq_l)
     ra, rb = folded(sq_r)
-    start_sum(1, sent_sum(
+    scatter(sent_sum(
         acc[...], jnp.concatenate([la, lb], axis=1), jnp.concatenate([rb, ra], axis=1)
     ))
     for c in range(PRE):
         turn_left(c, w, ql, own_l)
         turn_right(c, w, qr, own_r)
-    sum_sent(0)
+    gather()
+    for c in range(CHUNKS - LATE, CHUNKS):
+        forward(c)
+    sum_sent()
     for side in range(2):
         arrived((own_l, own_r)[side].at[pl.ds(PRE, CHUNKS - PRE)], mv_send.at[side])
     arrived(w.at[pl.ds(0, 2 * PRE * ch)], raw_send)
-    arrived(c_prev, c_send.at[0])
-    exchange(1, corr_of(end_sum(1)))
+    arrived(c_both, c_send)
 
     none = jnp.zeros((64, 256), BF)
 
@@ -347,8 +426,9 @@
 
     def finish(side, first):
         from_l, from_r = ((far_l, own_r), (own_l, far_r))[side]
-        arrived((c_prev, c_next)[side].at[1], c_recv.at[1, side])
-        corr = unpacked((c_prev, c_next)[side][1].astype(F32))
+        total = (tot_prev, tot_next)[side]
+        arrived(total, tot_recv.at[side])
+        corr = corr_of(total[...].astype(F32))
         keep_last(wl, *(left_columns, right_columns)[side](corr, scale_of(corr)))
         arrived((far_l, far_r)[side], far_recv.at[side])
         outer = (pl.ds(0, 128), pl.ds(256, 128))[side]
@@ -381,15 +461,16 @@
         finish(0, True)
         finish(1, False)
 
-    sum_sent(1)
+    gathered()
     arrived(in_l, mv_send.at[2])
     arrived(in_r, mv_send.at[3])
-    arrived(c_prev, c_send.at[1])
 
 
 def local(nx, ny, npos, latent):
     rows = latent.shape[0]
     g = rows // CHUNKS // 2
+    plane = nx * ny
+    slots, rest = divmod(SUM // TILE, plane)
     block = pltpu.VMEM((CHUNKS, 3 * g, 128), BF)
     return pl.pallas_call(
         functools.partial(kernel, nx, ny, npos),
@@ -408,19 +489,29 @@
             pltpu.VMEM((2, 512, 256), BF),
             pltpu.VMEM((BLK, 256), F32),
             pltpu.VMEM((2, 2, SUM, 128), BF),
-            pltpu.VMEM((2, 2, max(nx, ny) - 1, SUM, 128), BF),
+            pltpu.VMEM((2, max(nx, ny) - 1, SUM, 128), BF),
+            pltpu.VMEM((PACK, 128), BF),
             pltpu.VMEM((2, PACK, 128), BF),
-            pltpu.VMEM((2, PACK, 128), BF),
-            pltpu.VMEM((2, PACK, 128), BF),
+            pltpu.VMEM((slots, plane - 1, TILE, 128), BF),
+            pltpu.VMEM((plane - 1, TILE, 128), BF),
+            pltpu.VMEM((slots + 1, TILE, 128), BF),
+            pltpu.VMEM((SUM, 128), BF),
+            pltpu.VMEM((SUM, 128), BF),
             pltpu.SemaphoreType.DMA((LOADS,)),
-            pltpu.SemaphoreType.DMA((2, 2, len(PIECES))),
-            pltpu.SemaphoreType.DMA((2, 2, len(PIECES))),
+            pltpu.SemaphoreType.DMA((2, len(PIECES))),
+            pltpu.SemaphoreType.DMA((2, len(PIECES))),
             pltpu.SemaphoreType.DMA((4,)),
             pltpu.SemaphoreType.DMA((2, CHUNKS - PRE)),
             pltpu.SemaphoreType.DMA((2,)),
+            pltpu.SemaphoreType.DMA,
             pltpu.SemaphoreType.DMA((2,)),
-            pltpu.SemaphoreType.DMA((2, 2)),
             pltpu.SemaphoreType.DMA,
+            pltpu.SemaphoreType.DMA((2,)),
+            pltpu.SemaphoreType.DMA,
+            pltpu.SemaphoreType.DMA,
+            pltpu.SemaphoreType.DMA((max(rest, 1),)),
+            pltpu.SemaphoreType.DMA,
+            pltpu.SemaphoreType.DMA((slots + 1, 2)),
             pltpu.SemaphoreType.DMA((2,)),
         ],
         compiler_params=pltpu.CompilerParams(

time: 39.6 us -> 39.8 us (level)
  no operation moved by 1% of the time
where the time goes in v4:
time: 39.8 us; the launch traced here: 39.7 us
  Pallas kernels  38.5 us (97%)
  local copies, waits for them, and re-layouts  1.15 us (3%)
    pallas_call x1, Pallas kernels, local(): pl.pallas_call(functools.partial(kernel, nx, ny, npos), out_shape=jax.Sha...  38.5 us
    unnamed x1, local copies, waits for them, and re-layouts  1.15 us

profile of v4, /device:TPU:1, one launch (start us, length us, event | category | flops | bytes accessed | tf_op | source)
XLA Modules:
  0.0 39.7 jit_solution(6142794254674836560)
XLA Ops:
  0.0 38.5 %shard_map.17 = bf16[2048,384]{1,0:T(8,128)(2,1)S(1)} custom-call(bf16[2048,384]{1,0:T(8,128)(2,1)} %w_hbm.1), custom_call_target="tpu_custom_call" | custom-call | tf_op jit(solution)/shard_map/pallas_call | solution.py:475
  38.5 1.1 %copy.3 = bf16[2048,384]{1,0:T(8,128)(2,1)} copy(bf16[2048,384]{1,0:T(8,128)(2,1)S(1)} %shard_map.17) | data formatting | bytes 3145728

commit v5 on v4

--- a/solution.py
+++ b/solution.py
@@ -15,10 +15,10 @@
 CHUNKS = 8
 PRE = 4
 PACK = 288
-SUM = 304
+SUM = 320
 PIECES = ((0, 0, 144), (1, 144, 160))
 LOADS = 4
-TILE = 16
+TILE = 32
 LATE = 2
 MESH = pl.DeviceIdType.MESH
 
@@ -141,9 +141,9 @@
 def kernel(
     nx, ny, npos,
     w_hbm, out_v,
-    w, own_l, own_r, in_l, in_r, far_l, far_r, raw_l, raw_r,
+    w, own_l, own_r, in_l, in_r, far_l, far_r, raw,
     ql, qr, pql, nqr, wl, acc, part, got, c_own, c_both,
-    tile_got, rest_got, sums, tot_prev, tot_next,
+    tile_got, rest_got, sums, everyone, tot_prev, tot_next,
     load_sem, sum_send, sum_recv, mv_send, in_recv, far_recv, c_send, c_recv, raw_send, raw_recv,
     tile_send, tile_recv, rest_send, rest_recv, spread_send, tot_recv,
 ):
@@ -160,6 +160,7 @@
         return (lax.rem(y + k, ny) * nx + x, p)
 
     ring = (nx, ny)
+    raw_l, raw_r = raw.at[0], raw.at[1]
     c_prev, c_next = c_both.at[0], c_both.at[1]
     peers = [along(a, k) for a in (0, 1) for k in range(1, ring[a])] + [(r, nxt), (r, prv)]
 
@@ -262,7 +263,8 @@
                 remote(src, tot_prev.at[tile(n)], send.at[0], tot_recv.at[0], (peer_at[k], nxt))
                 remote(src, tot_next.at[tile(n)], send.at[1], tot_recv.at[1], (peer_at[k], prv))
 
-        arrived(tile_got, tile_recv)
+        if slots:
+            arrived(tile_got, tile_recv)
         for s in range(slots):
             n = s * plane + r
             total = part[1, 0, tile(n)].astype(F32)
@@ -282,20 +284,20 @@
             spread(sums.at[slots], n, spread_send.at[slots])
 
     def gathered():
-        everyone = pl.ds(0, plane * TILE)
         for j in range(rest):
             @pl.when(r != j)
             def _():
                 arrived(final.at[tile(slots * plane + j)], rest_send.at[j])
-        arrived(tile_got, tile_send)
+        if slots:
+            arrived(tile_got, tile_send)
         for s in range(slots):
             for side in range(2):
-                arrived(tot_prev.at[everyone], spread_send.at[s, side])
+                arrived(everyone, spread_send.at[s, side])
 
         @pl.when(r < rest)
         def _():
             for side in range(2):
-                arrived(tot_prev.at[everyone], spread_send.at[slots, side])
+                arrived(everyone, spread_send.at[slots, side])
 
     def forward(c):
         remote(in_l.at[c], far_l.at[c], mv_send.at[2], far_recv.at[0], (r, nxt))
@@ -316,7 +318,8 @@
         dst[c, 2 * g :] = (a[:, :128] + b[:, :128]).astype(BF)
 
     early = pl.ds(0, PRE * ch)
-    for c in range(PRE * ch // piece):
+    first_loads = -(-PRE * ch // piece)
+    for c in range(first_loads):
         loads[c].wait()
     pl.semaphore_wait(barrier, len(peers))
     remote(w.at[early], raw_l, raw_send, raw_recv.at[0], (r, nxt))
@@ -324,7 +327,7 @@
 
     sq = jnp.zeros((8, WIDE), F32)
     for c in range(LOADS):
-        if c * piece >= PRE * ch:
+        if c >= first_loads:
             loads[c].wait()
         block = w[pl.ds(c * piece, piece)]
         new = dot_tn(block[:, :256], block[:, 128:])[:BLK]
@@ -406,7 +409,7 @@
     sum_sent()
     for side in range(2):
         arrived((own_l, own_r)[side].at[pl.ds(PRE, CHUNKS - PRE)], mv_send.at[side])
-    arrived(w.at[pl.ds(0, 2 * PRE * ch)], raw_send)
+    arrived(raw, raw_send)
     arrived(c_both, c_send)
 
     none = jnp.zeros((64, 256), BF)
@@ -432,17 +435,17 @@
         keep_last(wl, *(left_columns, right_columns)[side](corr, scale_of(corr)))
         arrived((far_l, far_r)[side], far_recv.at[side])
         outer = (pl.ds(0, 128), pl.ds(256, 128))[side]
-        for c in range(0, CHUNKS, 4):
+        for c in range(0, CHUNKS, CHUNKS):
             for half in range(2):
                 a_of, b_of = pl.ds(half * g, g), pl.ds(2 * g, g)
                 terms = jnp.concatenate([
                     jnp.concatenate(
                         [from_l[n, a_of], from_l[n, b_of], from_r[n, b_of], from_r[n, a_of]], axis=1
                     )
-                    for n in range(c, c + 4)
+                    for n in range(c, c + CHUNKS)
                 ], axis=0)
                 a = dot(terms, wl[half])
-                for n in range(4):
+                for n in range(CHUNKS):
                     rows_of = pl.ds((c + n) * ch + half * g, g)
                     pair = a[n * g : n * g + g, :128], a[n * g : n * g + g, 128:]
                     out_v[rows_of, outer] = pair[side].astype(BF)
@@ -480,8 +483,7 @@
         scratch_shapes=[
             pltpu.VMEM((rows, WIDE), BF),
             block, block, block, block, block, block,
-            pltpu.VMEM((PRE * 2 * g, WIDE), BF),
-            pltpu.VMEM((PRE * 2 * g, WIDE), BF),
+            pltpu.VMEM((2, PRE * 2 * g, WIDE), BF),
             pltpu.VMEM((2, WIDE, 256), BF),
             pltpu.VMEM((2, WIDE, 256), BF),
             pltpu.VMEM((2, WIDE, 256), BF),
@@ -492,9 +494,10 @@
             pltpu.VMEM((2, max(nx, ny) - 1, SUM, 128), BF),
             pltpu.VMEM((PACK, 128), BF),
             pltpu.VMEM((2, PACK, 128), BF),
-            pltpu.VMEM((slots, plane - 1, TILE, 128), BF),
+            pltpu.VMEM((max(slots, 1), plane - 1, TILE, 128), BF),
             pltpu.VMEM((plane - 1, TILE, 128), BF),
             pltpu.VMEM((slots + 1, TILE, 128), BF),
+            pltpu.VMEM((plane, TILE, 128), BF),
             pltpu.VMEM((SUM, 128), BF),
             pltpu.VMEM((SUM, 128), BF),
             pltpu.SemaphoreType.DMA((LOADS,)),

time: 39.8 us -> 39 us (0.980)
  Pallas kernels: 38.5 us -> 37.8 us
    pallas_call x1, Pallas kernels: 38.5 us -> 37.8 us  [local(): pl.pallas_call(functools.partial(kernel, nx, ny, npos), out_shape=jax.Sha...]
where the time goes in v5:
time: 39 us; the launch traced here: 38.9 us
  Pallas kernels  37.8 us (97%)
  local copies, waits for them, and re-layouts  1.15 us (3%)
    pallas_call x1, Pallas kernels, local(): pl.pallas_call(functools.partial(kernel, nx, ny, npos), out_shape=jax.Sha...  37.8 us
    unnamed x1, local copies, waits for them, and re-layouts  1.15 us

profile of v5, /device:TPU:1, one launch (start us, length us, event | category | flops | bytes accessed | tf_op | source)
XLA Modules:
  0.0 38.9 jit_solution(8782777212349196417)
XLA Ops:
  0.0 37.8 %shard_map.17 = bf16[2048,384]{1,0:T(8,128)(2,1)S(1)} custom-call(bf16[2048,384]{1,0:T(8,128)(2,1)} %w_hbm.1), custom_call_target="tpu_custom_call" | custom-call | tf_op jit(solution)/shard_map/pallas_call | solution.py:478
  37.8 1.1 %copy.3 = bf16[2048,384]{1,0:T(8,128)(2,1)} copy(bf16[2048,384]{1,0:T(8,128)(2,1)S(1)} %shard_map.17) | data formatting | bytes 3145728

commit v6 on v5

--- a/solution.py
+++ b/solution.py
@@ -261,6 +261,7 @@
         def spread(src, n, send):
             for k in range(plane):
                 remote(src, tot_prev.at[tile(n)], send.at[0], tot_recv.at[0], (peer_at[k], nxt))
+            for k in range(plane):
                 remote(src, tot_next.at[tile(n)], send.at[1], tot_recv.at[1], (peer_at[k], prv))
 
         if slots:

time: 39 us -> 39 us (level)
  no operation moved by 1% of the time
where the time goes in v6:
time: 39 us; the launch traced here: 38.9 us
  Pallas kernels  37.7 us (97%)
  local copies, waits for them, and re-layouts  1.15 us (3%)
    pallas_call x1, Pallas kernels, local(): pl.pallas_call(functools.partial(kernel, nx, ny, npos), out_shape=jax.Sha...  37.7 us
    unnamed x1, local copies, waits for them, and re-layouts  1.15 us

profile of v6, /device:TPU:1, one launch (start us, length us, event | category | flops | bytes accessed | tf_op | source)
XLA Modules:
  0.0 38.9 jit_solution(11227608360260707886)
XLA Ops:
  0.0 37.7 %shard_map.17 = bf16[2048,384]{1,0:T(8,128)(2,1)S(1)} custom-call(bf16[2048,384]{1,0:T(8,128)(2,1)} %w_hbm.1), custom_call_target="tpu_custom_call" | custom-call | tf_op jit(solution)/shard_map/pallas_call | solution.py:479
  37.8 1.1 %copy.3 = bf16[2048,384]{1,0:T(8,128)(2,1)} copy(bf16[2048,384]{1,0:T(8,128)(2,1)S(1)} %shard_map.17) | data formatting | bytes 3145728
